TPU v7x, 32 devices: a whole 2x2x4 slice. The times are simulated.
32 devices in a mesh: ctx: 16 (over z, y, core), wt: 2 (over x).
Axes of the slice: x: 2, y: 2, z: 4, core: 2. Of those that a mesh axis runs over, the one named last changes fastest.
Arguments:
- block_input: bfloat16 [2, 2048, 896], P('wt', 'ctx'), may hold values from -40 to 40
- cotangent: bfloat16 [2, 2048, 896], P('wt', 'ctx'), may hold values from -6 to 6
- norm_attn: float32 [896], replicated, may hold values from 0.1 to 1.9
- w_qkv: bfloat16 [896, 1152], P('wt'), may hold values from -1 to 1
- b_qkv: float32 [1152], replicated, may hold values from -3 to 3
- w_out: bfloat16 [896, 896], P('wt'), may hold values from -3 to 3
- norm_mlp: float32 [896], replicated, may hold values from 0.1 to 1.9
- w_gate: bfloat16 [896, 4864], P('wt'), may hold values from -0.1875 to 0.1875
- w_up: bfloat16 [896, 4864], P('wt'), may hold values from -0.1875 to 0.1875
- w_down: bfloat16 [4864, 896], P('wt'), may hold values from -0.078125 to 0.078125
Outputs:
- block_output: bfloat16 [2, 2048, 896], P('wt', 'ctx')
- grad_input: float32 [2, 2048, 896], P('wt', 'ctx')
- grad_norm_attn: float32 [896], P(('ctx', 'wt'))
- grad_w_qkv: float32 [896, 1152], P(('ctx', 'wt'))
- grad_b_qk: float32 [1024], P(('ctx', 'wt'))
- grad_b_v: float32 [128], P(('ctx', 'wt'))
- grad_w_out: float32 [896, 896], P(('ctx', 'wt'))
- grad_norm_mlp: float32 [896], P(('ctx', 'wt'))
- grad_w_gate: float32 [896, 4864], P(('ctx', 'wt'))
- grad_w_up: float32 [896, 4864], P(('ctx', 'wt'))
- grad_w_down: float32 [4864, 896], P(('ctx', 'wt'))
All inputs are finite; a program needn't handle non-finite values.
Results may differ from a plain program's by a relative error of at most 0.035.
Values may be sent and summed in bfloat16 or wider, within the bound.
No kernel may reach another device: no remote copies, remote signals or barrier semaphores. Data moves between devices by JAX's collectives and lax.ppermute only.
A program may use at most 320 MiB of HBM per device.

v0:
```python
import functools
import math

import jax
import jax.numpy as jnp
from jax import lax
from jax.experimental import pallas as pl
from jax.experimental.pallas import tpu as pltpu
from jax.sharding import Mesh
from jax.sharding import PartitionSpec as P

KVH = 2
HD = 64
EPSILON = 1e-06
THETA = 1000000.0
F32 = jnp.float32
BF = jnp.bfloat16
CTX = ("group", "chip", "core")


def rms_norm(hidden, gain):
    inverse = lax.rsqrt(jnp.mean(hidden * hidden, axis=-1, keepdims=True) + EPSILON)
    return (hidden * inverse * gain, inverse)


def norm_back(grad_normed, hidden, inverse, gain):
    scaled = grad_normed * gain
    return inverse * (
        scaled - hidden * inverse * inverse * jnp.mean(scaled * hidden, axis=-1, keepdims=True)
    )


def after(value, done):
    return lax.optimization_barrier((value, done))[0]


def gate_kernel(value_ref, done_ref, out_ref):
    pass


def gate(value, done):
    any_spec = pl.BlockSpec(memory_space=pl.ANY)
    return pl.pallas_call(
        gate_kernel,
        out_shape=jax.ShapeDtypeStruct(value.shape, value.dtype),
        in_specs=[any_spec, any_spec],
        out_specs=any_spec,
        input_output_aliases={0: 0},
        name="gate",
    )(value, done)


def dot(a, b, ca=1, cb=0, out=F32):
    return lax.dot_general(a, b, (((ca,), (cb,)), ((), ())), preferred_element_type=out)


def kdot(a, b, ca, cb, precision=None):
    return lax.dot_general(
        a, b, (((ca,), (cb,)), ((), ())), preferred_element_type=F32, precision=precision
    )


def head_rows(ref, sel, head, blk):
    return ref[sel * blk : (sel + 1) * blk, head * HD : (head + 1) * HD]


def diag_mask(blk, groups, flip):
    shape = (blk, groups * blk)
    key = lax.broadcasted_iota(jnp.int32, shape, 0)
    query = lax.broadcasted_iota(jnp.int32, shape, 1) % blk
    half = blk // 2
    key = jnp.where(flip, (key + half) % blk, key)
    query = jnp.where(flip, (query + half) % blk, query)
    return key <= query


def fwd_kernel(pairs, groups, blk, idx_ref, q_ref, *refs):
    kv_refs = refs[:pairs]
    att_ref, lse_ref, kv_all, qp, scores, acc = refs[pairs:]
    here = idx_ref[0]
    core = idx_ref[1]
    width = groups * blk
    for k in range(pairs):
        kv_all[k] = kv_refs[k][...]
    zeros = jnp.zeros((blk, HD), BF)
    for sel in range(2):
        for head in range(groups):
            qp[sel, head * blk : (head + 1) * blk, :] = jnp.concatenate(
                [head_rows(q_ref, sel, head, blk), zeros], axis=1
            )

    def kv_block(low_high, j):
        return kv_all[j ^ here, pl.ds(pl.multiple_of(low_high * blk, blk), blk), :]

    def fold(top, s):
        return jnp.maximum(top, jnp.max(s.reshape(blk // 8, 8, width), axis=0))

    start = jnp.full((8, width), -1e30, F32)

    def full_step(j, top):
        s = kdot(kv_block(0, j), qp[1], 1, 1)
        scores[j] = s
        return fold(top, s)

    top_high = lax.fori_loop(0, pairs, full_step, start)

    def off_step(u, tops):
        low = u < here
        j = jnp.where(low, u, u + 1)
        sel = jnp.where(low, 0, 1)
        s = kdot(kv_block(sel, j), qp[sel], 1, 1)
        scores[pairs + u] = s
        m = jnp.max(s.reshape(blk // 8, 8, width), axis=0)
        return (
            jnp.where(low, jnp.maximum(tops[0], m), tops[0]),
            jnp.where(low, tops[1], jnp.maximum(tops[1], m)),
        )

    tops = lax.fori_loop(0, pairs - 1, off_step, (start, top_high))
    tops = list(tops)
    for sel in range(2):
        mask = diag_mask(blk, groups, (core == 1) if sel == 0 else (core == 0))
        s = jnp.where(mask, kdot(kv_block(sel, here), qp[sel], 1, 1), -1e30)
        scores[2 * pairs - 1 + sel] = s
        tops[sel] = jnp.max(fold(tops[sel], s), axis=0, keepdims=True)

    def probs(s, top):
        p = jnp.exp(s - top)
        return p.astype(BF), jnp.sum(p.reshape(blk // 8, 8, width), axis=0)

    totals = []
    for sel in range(2):
        pb, t = probs(scores[2 * pairs - 1 + sel], tops[sel])
        acc[sel] = kdot(kv_block(sel, here), pb, 0, 0)
        totals.append(t)

    def full_mix(j, total):
        pb, t = probs(scores[j], tops[1])
        acc[1] += kdot(kv_block(0, j), pb, 0, 0)
        return total + t

    totals[1] = lax.fori_loop(0, pairs, full_mix, totals[1])

    def off_mix(u, totals):
        low = u < here
        j = jnp.where(low, u, u + 1)
        sel = jnp.where(low, 0, 1)
        pb, t = probs(scores[pairs + u], jnp.where(low, tops[0], tops[1]))
        acc[sel] += kdot(kv_block(sel, j), pb, 0, 0)
        return (
            jnp.where(low, totals[0] + t, totals[0]),
            jnp.where(low, totals[1], totals[1] + t),
        )

    totals = lax.fori_loop(0, pairs - 1, off_mix, tuple(totals))
    for sel in range(2):
        total = jnp.sum(totals[sel], axis=0, keepdims=True)
        lse_ref[sel] = tops[sel] + jnp.log(total)
        mixed = acc[sel, HD:, :] / total
        for head in range(groups):
            att_ref[sel * blk : (sel + 1) * blk, head * HD : (head + 1) * HD] = (
                mixed[:, head * blk : (head + 1) * blk].T.astype(BF)
            )


def bwd_kernel(
    pairs, groups, blk, scale, idx_ref, q_ref, do_ref, att_ref, lse_ref, rope_ref, *refs
):
    kv_refs = refs[:pairs]
    gq_ref, gsum_ref = refs[pairs : pairs + 2]
    dkv_refs = refs[pairs + 2 : 2 * pairs + 2]
    kv_all, qp, dop, dkv, dq_acc = refs[2 * pairs + 2 :]
    here = idx_ref[0]
    core = idx_ref[1]
    for k in range(pairs):
        kv_all[k] = kv_refs[k][...]
    zeros = jnp.zeros((blk, HD), BF)
    for sel in range(2):
        for head in range(groups):
            rows = slice(head * blk, (head + 1) * blk)
            qp[sel, rows, :] = jnp.concatenate([head_rows(q_ref, sel, head, blk), zeros], axis=1)
            dop[sel, rows, :] = jnp.concatenate([zeros, head_rows(do_ref, sel, head, blk)], axis=1)
    prod = do_ref[...].astype(F32) * att_ref[...].astype(F32)
    picks_shape = (8, groups * HD)
    picks = (
        lax.broadcasted_iota(jnp.int32, picks_shape, 1) // HD
        == lax.broadcasted_iota(jnp.int32, picks_shape, 0)
    ).astype(F32)
    delta_heads = kdot(picks, prod, 1, 1, lax.Precision.HIGHEST)
    deltas = [
        jnp.concatenate(
            [delta_heads[h : h + 1, sel * blk : (sel + 1) * blk] for h in range(groups)], axis=1
        )
        for sel in range(2)
    ]
    lses = [lse_ref[0], lse_ref[1]]

    def kv_block(low_high, j):
        return kv_all[j ^ here, pl.ds(pl.multiple_of(low_high * blk, blk), blk), :]

    def terms(kv, sel, lse, delta, mask=None):
        s = kdot(kv, qp[sel], 1, 1)
        p = jnp.exp(s - lse) if mask is None else jnp.where(
            mask, jnp.exp(jnp.where(mask, s, -1e30) - lse), 0.0
        )
        dp = kdot(kv, dop[sel], 1, 1)
        ds = (p * (dp - delta)).astype(BF)
        pb = p.astype(BF)
        dk = kdot(ds, qp[sel], 1, 0) + kdot(pb, dop[sel], 1, 0)
        return ds, dk

    for sel in range(2):
        mask = diag_mask(blk, groups, (core == 1) if sel == 0 else (core == 0))
        kv = kv_block(sel, here)
        ds, dk = terms(kv, sel, lses[sel], deltas[sel], mask)
        dq_acc[sel] = kdot(kv, ds, 0, 0)
        dkv[here, sel] = dk

    def full_step(j, carry):
        kv = kv_block(0, j)
        ds, dk = terms(kv, 1, lses[1], deltas[1])
        dq_acc[1] += kdot(kv, ds, 0, 0)

        @pl.when(j == here)
        def _():
            dkv[j, 0] += dk

        @pl.when(j != here)
        def _():
            dkv[j, 0] = dk

        return carry

    lax.fori_loop(0, pairs, full_step, 0)

    def off_step(u, carry):
        low = u < here
        j = jnp.where(low, u, u + 1)
        sel = jnp.where(low, 0, 1)
        kv = kv_block(sel, j)
        ds, dk = terms(
            kv, sel, jnp.where(low, lses[0], lses[1]), jnp.where(low, deltas[0], deltas[1])
        )
        dq_acc[sel] += kdot(kv, ds, 0, 0)

        @pl.when(low)
        def _():
            dkv[j, 0] += dk
            dkv[j, 1] = jnp.zeros_like(dk)

        @pl.when(jnp.logical_not(low))
        def _():
            dkv[j, 1] = dk

        return carry

    lax.fori_loop(0, pairs - 1, off_step, 0)
    for k in range(pairs):
        for sel in range(2):
            dkv_refs[k][sel * blk : (sel + 1) * blk, :] = dkv[k ^ here, sel].astype(
                dkv_refs[k].dtype
            )
    for head in range(groups):
        cols = slice(head * HD, (head + 1) * HD)
        total = jnp.zeros((1, HD), F32)
        for sel in range(2):
            rows = slice(sel * blk, (sel + 1) * blk)
            cosine = rope_ref[0, :, rows]
            sine = rope_ref[1, :, rows]
            turned = dq_acc[sel, :HD, head * blk : (head + 1) * blk] * scale
            low, high = turned[: HD // 2], turned[HD // 2 :]
            back = jnp.concatenate(
                [low * cosine + high * sine, high * cosine - low * sine], axis=0
            ).T
            gq_ref[rows, cols] = back.astype(BF)
            total = total + jnp.sum(back, axis=0, keepdims=True)
        gsum_ref[:, cols] = total


VMEM_SPEC = pl.BlockSpec(memory_space=pltpu.VMEM)
SMEM_SPEC = pl.BlockSpec(memory_space=pltpu.SMEM)


def attention_fwd(idx, q, kvs):
    pairs = len(kvs)
    rows, cols = q.shape
    blk = rows // 2
    groups = cols // HD
    width = groups * blk
    return pl.pallas_call(
        functools.partial(fwd_kernel, pairs, groups, blk),
        out_shape=(
            jax.ShapeDtypeStruct((rows, cols), BF),
            jax.ShapeDtypeStruct((2, 1, width), F32),
        ),
        in_specs=[SMEM_SPEC] + [VMEM_SPEC] * (1 + pairs),
        out_specs=(VMEM_SPEC, VMEM_SPEC),
        scratch_shapes=[
            pltpu.VMEM((pairs, rows, 2 * HD), BF),
            pltpu.VMEM((2, width, 2 * HD), BF),
            pltpu.VMEM((2 * pairs + 1, blk, width), F32),
            pltpu.VMEM((2, 2 * HD, width), F32),
        ],
        compiler_params=pltpu.CompilerParams(vmem_limit_bytes=56 * 2**20),
        name="attn_fwd",
    )(idx, q, *kvs)


def attention_bwd(idx, q, d_out, att, lse, rope_t, kvs):
    pairs = len(kvs)
    rows, cols = q.shape
    blk = rows // 2
    groups = cols // HD
    width = groups * blk
    res = pl.pallas_call(
        functools.partial(bwd_kernel, pairs, groups, blk, 1.0 / math.sqrt(HD)),
        out_shape=(jax.ShapeDtypeStruct((rows, cols), BF), jax.ShapeDtypeStruct((1, cols), F32))
        + tuple(jax.ShapeDtypeStruct((rows, 2 * HD), BF) for _ in range(pairs)),
        in_specs=[SMEM_SPEC] + [VMEM_SPEC] * (5 + pairs),
        out_specs=(VMEM_SPEC,) * (2 + pairs),
        scratch_shapes=[
            pltpu.VMEM((pairs, rows, 2 * HD), BF),
            pltpu.VMEM((2, width, 2 * HD), BF),
            pltpu.VMEM((2, width, 2 * HD), BF),
            pltpu.VMEM((pairs, 2, blk, 2 * HD), F32),
            pltpu.VMEM((2, 2 * HD, width), F32),
        ],
        compiler_params=pltpu.CompilerParams(vmem_limit_bytes=56 * 2**20),
        name="attn_bwd",
    )(idx, q, d_out, att, lse, rope_t, *kvs)
    return res[0], res[1], res[2:]


def columns_kernel(groups_z, ff_blk, ff_wide, window, rows, idx_ref, gate_ref, up_ref, out_ref, win, sems):
    ff = gate_ref.shape[1]
    here = idx_ref[0]
    shifts = []
    copies = []
    for m, ref in enumerate((gate_ref, up_ref)):
        for g in range(groups_z):
            col = (g * 8 + here) * ff_blk
            start = jnp.minimum((col // 128) * 128, ff - window)
            if m == 0:
                shifts.append(col - start)
            copies.append(
                pltpu.make_async_copy(
                    ref.at[
                        pl.ds(pl.multiple_of(idx_ref[1] * rows, 16), rows),
                        pl.ds(pl.multiple_of(start, 128), window),
                    ],
                    win.at[m * groups_z + g],
                    sems.at[m * groups_z + g],
                )
            )
    for copy in copies:
        copy.start()
    for m in range(2):
        pieces = [None] * (ff_wide // 128)
        for g in range(groups_z):
            first = g * ff_blk // 128
            lead = g * ff_blk - first * 128
            tiles = -(-(lead + ff_blk) // 128)
            copies[m * groups_z + g].wait()
            row = lax.broadcasted_iota(jnp.int32, (window, tiles * 128), 0)
            lane = lax.broadcasted_iota(jnp.int32, (window, tiles * 128), 1) - lead
            hot = jnp.logical_and(row == lane + shifts[g], jnp.logical_and(lane >= 0, lane < ff_blk))
            part = kdot(win[m * groups_z + g], hot.astype(F32).astype(BF), 1, 0)
            for t in range(tiles):
                tile = part[:, t * 128 : (t + 1) * 128]
                old = pieces[first + t]
                pieces[first + t] = tile if old is None else old + tile
        for t, tile in enumerate(pieces):
            col = m * ff_wide + t * 128
            out_ref[:, col : col + 128] = (
                jnp.zeros((out_ref.shape[0], 128), BF) if tile is None else tile.astype(BF)
            )


def hidden_columns(idx, gate, up, groups_z, ff_blk, ff_wide, rows):
    ff = gate.shape[1]
    window = min(-(-(ff_blk + 127) // 128) * 128, ff)
    return pl.pallas_call(
        functools.partial(columns_kernel, groups_z, ff_blk, ff_wide, window, rows),
        out_shape=jax.ShapeDtypeStruct((rows, 2 * ff_wide), BF),
        in_specs=[SMEM_SPEC, pl.BlockSpec(memory_space=pl.ANY), pl.BlockSpec(memory_space=pl.ANY)],
        out_specs=VMEM_SPEC,
        scratch_shapes=[
            pltpu.VMEM((2 * groups_z, rows, window), BF),
            pltpu.SemaphoreType.DMA((2 * groups_z,)),
        ],
        name="hidden_columns",
    )(idx, gate, up)


def mlp_kernel(idx_ref, *refs):
    n2_refs, cot_refs = refs[:8], refs[8:16]
    gu_refs, down_refs = refs[16:19], refs[19:22]
    keep_ref, send_ref, g_ref, act_ref, n2_all, cot_all, down_w = refs[22:29]
    gu_w = refs[29]
    wt = idx_ref[0]
    odd = idx_ref[1]
    tok = n2_refs[0].shape[0]
    wide = gu_w.shape[1] // 2
    down_half = down_refs[0].shape[0]
    for k in range(8):
        n2_all[k * tok : (k + 1) * tok, :] = n2_refs[k][...]
        cot_all[k * tok : (k + 1) * tok, :] = cot_refs[k][...]
    for full, (own, first, second) in ((gu_w, gu_refs), (down_w, down_refs)):
        half, quarter = own.shape[0], first.shape[0]
        for w in range(2):

            @pl.when(wt == w)
            def _():
                full[w * half : (w + 1) * half, :] = own[...]

            other = (1 - w) * half
            for z in range(2):

                @pl.when(jnp.logical_and(wt == w, odd == z))
                def _():
                    at = other + z * quarter
                    full[at : at + quarter, :] = first[...]
                    at = other + (1 - z) * quarter
                    full[at : at + quarter, :] = second[...]

    pad = wide - 2 * down_half
    if pad:
        down_w[2 * down_half :, :] = jnp.zeros((pad, down_w.shape[1]), BF)

    def chunk(start, out_ref, out_start):
        rows = pl.ds(start, 2 * tok)
        n2 = n2_all[rows, :]
        gate = kdot(n2, gu_w[:, :wide], 1, 0)
        up = kdot(n2, gu_w[:, wide:], 1, 0)
        grad_act = kdot(cot_all[rows, :], down_w[...], 1, 1)
        sig = jax.nn.sigmoid(gate)
        gated = gate * sig
        act_ref[rows, :] = (gated * up).astype(BF)
        g_gate = (grad_act * up * sig * (1.0 + gate * (1.0 - sig))).astype(BF)
        g_up = (grad_act * gated).astype(BF)
        g_ref[rows, :wide] = g_gate
        g_ref[rows, wide:] = g_up
        grad = kdot(g_gate, gu_w[:, :wide], 1, 1) + kdot(g_up, gu_w[:, wide:], 1, 1)
        out_ref[pl.ds(out_start, 2 * tok), :] = grad.astype(out_ref.dtype)

    for j in range(2):
        chunk(2 * tok * (2 + j), send_ref, 2 * tok * j)
    for j in range(2):
        chunk(2 * tok * j, keep_ref, 2 * tok * j)


def mlp(idx, n2, cot, gu, down):
    tok, dim = n2[0].shape
    wide2 = gu[0].shape[1]
    wide = wide2 // 2
    sds = jax.ShapeDtypeStruct
    return pl.pallas_call(
        mlp_kernel,
        out_shape=(
            sds((4 * tok, dim), F32),
            sds((4 * tok, dim), BF),
            sds((8 * tok, wide2), BF),
            sds((8 * tok, wide), BF),
            sds((8 * tok, dim), BF),
            sds((8 * tok, dim), BF),
            sds((wide, dim), BF),
        ),
        in_specs=[SMEM_SPEC] + [VMEM_SPEC] * 22,
        out_specs=(VMEM_SPEC,) * 7,
        scratch_shapes=[pltpu.VMEM((dim, wide2), BF)],
        compiler_params=pltpu.CompilerParams(vmem_limit_bytes=56 * 2**20),
        name="mlp",
    )(idx, *n2, *cot, *gu, *down)


def outer_kernel(blocks, idx_ref, att_ref, gh_ref, n1_ref, gq_ref, mine_ref, send_ref):
    half = gq_ref.shape[1]
    rows = mine_ref.shape[1] // 2
    upper = idx_ref[1] == 1
    second = idx_ref[0] == 1
    gh = jnp.where(upper, gh_ref[:, half:].astype(F32), gh_ref[:, :half].astype(F32)).astype(BF)
    for part, (left, right) in enumerate(((att_ref[...], gh), (n1_ref[...], gq_ref[...]))):
        full = kdot(left, right, 0, 0)
        cols = slice(part * half, (part + 1) * half)
        for b in range(blocks):
            low = full[2 * b * rows : (2 * b + 1) * rows]
            high = full[(2 * b + 1) * rows : (2 * b + 2) * rows]
            at = slice(b % 2 * rows, (b % 2 + 1) * rows)
            mine_ref[b // 2, at, cols] = jnp.where(second, high, low).astype(BF)
            send_ref[b // 2, at, cols] = jnp.where(second, low, high).astype(BF)


def outer_terms(idx, att, gh, n1, gq, blocks):
    dim = att.shape[1]
    shape = jax.ShapeDtypeStruct((blocks // 2, dim // blocks, 2 * gq.shape[1]), BF)
    return pl.pallas_call(
        functools.partial(outer_kernel, blocks),
        out_shape=(shape, shape),
        in_specs=[SMEM_SPEC] + [VMEM_SPEC] * 4,
        out_specs=(VMEM_SPEC, VMEM_SPEC),
        name="outer_terms",
    )(idx, att, gh, n1, gq)


def assemble_kernel(groups_z, ff_blk, ff_wide, factor, idx_ref, *refs):
    part_refs = refs[:8]
    gate_ref, up_ref, parts = refs[8:]
    for k in range(8):
        parts[k] = part_refs[k][...].astype(F32) * factor
    for plane in range(8):
        part = parts[plane ^ idx_ref[0]]
        for ref, start in ((gate_ref, 0), (up_ref, ff_wide)):
            for g in range(groups_z):
                col = (g * 8 + plane) * ff_blk
                ref[:, col : col + ff_blk] = part[:, start + g * ff_blk : start + (g + 1) * ff_blk]


def assemble(idx, parts, groups_z, ff_blk, ff_wide, factor):
    rows = parts[0].shape[0]
    shape = jax.ShapeDtypeStruct((rows, 8 * groups_z * ff_blk), F32)
    return pl.pallas_call(
        functools.partial(assemble_kernel, groups_z, ff_blk, ff_wide, factor),
        out_shape=(shape, shape),
        in_specs=[SMEM_SPEC] + [VMEM_SPEC] * 8,
        out_specs=(VMEM_SPEC, VMEM_SPEC),
        scratch_shapes=[pltpu.VMEM((8, rows, 2 * ff_wide), F32)],
        name="assemble",
    )(idx, *parts)


def shards(block_input, cotangent, norm_attn, w_qkv, b_qkv, w_out, norm_mlp, w_gate, w_up, w_down):
    ctx_count = lax.axis_size(CTX)
    groups_z = ctx_count // 4
    pairs = ctx_count // 2
    device_count = 2 * ctx_count
    z_bits = groups_z.bit_length() - 1
    _, tok, dim = block_input.shape
    half_tok = tok // 2
    length = tok * ctx_count
    half_dim = dim // 2
    kv_cols = KVH * HD
    ff = w_gate.shape[1]
    ff_blk = ff // device_count
    factor = 1.0 / math.sqrt(2 * length)
    ctx = lax.axis_index(CTX)
    wt = lax.axis_index("wt")
    core = ctx % 2
    chip_y = (ctx // 2) % 2
    pair = ctx // 2
    group = ctx // 4
    plane = (ctx % 4) * 2 + wt

    def swap_of(a, cx, wx):
        if wx == 0:
            return lax.ppermute(a, CTX, [(i, i ^ cx) for i in range(ctx_count)])
        if cx == 0:
            return lax.ppermute(a, "wt", [(0, 1), (1, 0)])
        return lax.ppermute(
            a, CTX + ("wt",), [(i, i ^ (2 * cx + wx)) for i in range(device_count)]
        )

    def by_bit(bit, first, second, axis):
        return jnp.where(
            bit == 0,
            jnp.concatenate([first, second], axis=axis),
            jnp.concatenate([second, first], axis=axis),
        )

    def pick(a, index, axis=0):
        return lax.dynamic_index_in_dim(a, index, axis, keepdims=False)

    def pair_rows(own, peer):
        return jnp.concatenate(
            [own[:half_tok], peer[:half_tok], own[half_tok:], peer[half_tok:]], axis=0
        )

    def own_rows(a):
        return jnp.concatenate([a[:half_tok], a[tok : tok + half_tok]], axis=0)

    def peer_rows(a):
        return jnp.concatenate([a[half_tok:tok], a[tok + half_tok :]], axis=0)

    head_cols = dim // KVH
    rope_cols = head_cols + HD

    def core_cols(a, axis):
        pieces = [
            (head_cols * core, head_cols),
            (dim + HD * core, HD),
            (dim + kv_cols + HD * core, HD),
        ]
        return jnp.concatenate(
            [lax.dynamic_slice_in_dim(a, s, w, axis) for s, w in pieces], axis=axis
        )

    wq_own = core_cols(w_qkv, 1)
    wq_recv = swap_of(wq_own, 0, 1)
    x_own = block_input[0]
    x_two = pair_rows(x_own, swap_of(x_own, 1, 0)).astype(F32)
    b_own = core_cols(b_qkv, 0)

    ff_own = groups_z * ff_blk
    ff_pad = -ff_own % 128
    ff_wide = ff_own + ff_pad

    def plane_gather(a, filler=None):
        four = [a, swap_of(a, 0, 1), swap_of(a, 2, 0), swap_of(a, 2, 1)]
        if filler is not None:
            four = [a] + [after(v, filler) for v in four[1:]]
        return four + [swap_of(v, 1, 0) for v in four]

    def plane_quad(keep, send):
        quad = keep.astype(F32) + swap_of(send, 1, 0).astype(F32)
        return quad.reshape(4, tok, dim)

    def plane_sends(quad):
        return [
            swap_of(quad[1].astype(BF), 0, 1),
            swap_of(quad[2].astype(BF), 2, 0),
            swap_of(quad[3].astype(BF), 2, 1),
        ]

    def plane_finish(quad, recv):
        return quad[0] + recv[0].astype(F32) + recv[1].astype(F32) + recv[2].astype(F32)

    def ff_cols(p, part, gate, up, rows):
        at = jnp.stack([p, part]).astype(jnp.int32)
        return hidden_columns(at, gate, up, groups_z, ff_blk, ff_wide, rows)

    w_out_l, cot_own = after(w_out, wq_own), after(cotangent[0], wq_own)
    wo_recv = swap_of(lax.dynamic_slice_in_dim(w_out_l, half_dim * core, half_dim, 1), 0, 1)
    cot_all = plane_gather(cot_own)

    z_odd = group & 1

    def z_next_of(a):
        return lax.ppermute(a, CTX, [(i, i ^ 4) for i in range(ctx_count)])

    normed1, inv1 = rms_norm(x_two, norm_attn)
    normed1_bf = normed1.astype(BF)
    wq = by_bit(wt, wq_own, wq_recv, 0)
    project = dot(normed1_bf, wq) + b_own
    within = jnp.arange(half_tok, dtype=jnp.int32)
    peer = ctx ^ 1
    pos = jnp.concatenate(
        [
            ctx * half_tok + within,
            peer * half_tok + within,
            length - (ctx + 1) * half_tok + within,
            length - (peer + 1) * half_tok + within,
        ]
    )
    steps = jnp.arange(HD // 2, dtype=F32)
    angles = pos.astype(F32)[:, None] * (THETA ** (-2.0 * steps / HD))[None, :]
    cosine = jnp.tile(jnp.cos(angles), (1, 2 * rope_cols // HD))
    sine = jnp.tile(jnp.sin(angles), (1, 2 * rope_cols // HD))

    def halves(u):
        first = (lax.broadcasted_iota(jnp.int32, (1, u.shape[1]), 1) % HD) < HD // 2
        return first, jnp.roll(u, -(HD // 2), axis=1), jnp.roll(u, HD // 2, axis=1)

    def rope(u):
        first, ahead, behind = halves(u)
        return u * cosine + jnp.where(first, -ahead, behind) * sine

    def unrope(g):
        cols = g.shape[1]
        first, ahead, behind = halves(g * sine[:, :cols])
        return g * cosine[:, :cols] + jnp.where(first, ahead, -behind)

    rotated = rope(project[:, :rope_cols]).astype(BF)
    q_scaled = rotated[:, :head_cols] * BF(1.0 / math.sqrt(HD))
    kv_own = jnp.concatenate([rotated[:, head_cols:], project[:, rope_cols:].astype(BF)], axis=1)
    kvs = [kv_own] + [swap_of(kv_own, 2 * k, 0) for k in range(1, pairs)]

    w_gate_l, w_up_l = after(w_gate, kv_own), after(w_up, kv_own)
    w_down_l = after(w_down, kv_own)
    down_shape = (groups_z // 2, 8, ff_blk, dim)
    gu_first = swap_of(ff_cols(plane ^ 1, z_odd, w_gate_l, w_up_l, half_dim // 2), 0, 1)
    down_peer = w_down_l.reshape(2, -1, 8, ff_blk, dim)
    down_peer = pick(pick(down_peer, plane ^ 1, 2), z_odd).reshape(-1, dim)
    down_first = swap_of(down_peer, 0, 1)
    gu_second = z_next_of(after(gu_first, kv_own))
    down_second = z_next_of(after(down_first, kv_own))
    down_own = pick(w_down_l.reshape(down_shape), plane, 1).reshape(-1, dim)
    idx = jnp.stack([pair, core]).astype(jnp.int32)
    att_heads, lse = attention_fwd(idx, q_scaled, kvs)
    att_peer = swap_of(att_heads, 1, 0)
    wo_other = by_bit(core, wo_recv, swap_of(after(wo_recv, att_heads), 1, 0), 1)
    wo = by_bit(wt, w_out, wo_other, 0)
    att_peer = pair_rows(peer_rows(att_peer), own_rows(att_peer))
    att_two = by_bit(core, att_heads, att_peer, 1)
    hidden1 = x_own.astype(F32) + dot(own_rows(att_two), wo)
    normed2, inv2 = rms_norm(hidden1, norm_mlp)
    normed2_bf = normed2.astype(BF)
    w_gate_l, w_up_l = after(w_gate, normed2_bf), after(w_up, normed2_bf)
    gu_own = ff_cols(plane, jnp.int32(0), w_gate_l, w_up_l, half_dim)
    n2 = plane_gather(normed2_bf, (gu_own, down_own))

    keep, send, g_gu, active, n2_all, cot_all, down_w = mlp(
        jnp.stack([wt, z_odd]).astype(jnp.int32),
        n2,
        cot_all,
        (gu_own, gu_first, gu_second),
        (down_own, down_first, down_second),
    )
    gn2_quad = plane_quad(keep, send)
    out_keep = dot(active[: 4 * tok], down_w, 1, 0, BF)
    out_send = dot(active[4 * tok :], down_w, 1, 0, BF)
    n2_l, active_l = after(n2_all, gn2_quad), after(active, gn2_quad)
    gw_down = dot(active_l, cot_all, 0, 0, BF)
    gw_gu = dot(n2_l, g_gu, 0, 0, BF)

    def z_half_send(a, bit):
        a = a.reshape((a.shape[0] // 2, 2) + a.shape[1:])
        mine_bit = (group >> bit) & 1
        send = pick(a, 1 - mine_bit, 1)
        mask = 4 << bit
        recv = lax.ppermute(send, CTX, [(i, i ^ mask) for i in range(ctx_count)])
        return pick(a, mine_bit, 1), recv

    def z_half_add(pair_of):
        return pair_of[0].astype(F32) + pair_of[1].astype(F32)

    def z_half_more(pair_of, done):
        for bit in range(1, z_bits):
            part = z_half_add((pair_of[0], after(pair_of[1], done))).astype(BF)
            pair_of = z_half_send(part, bit)
        return pair_of, part

    def z_half_last(pair_of, done):
        return z_half_add((pair_of[0], gate(pair_of[1], done)))[0]

    gn_recv = plane_sends(gn2_quad)
    gn_recv[0] = after(gn_recv[0], (gw_gu, gw_down))
    grad_norm2 = plane_finish(gn2_quad, gn_recv)
    z_gu = z_half_send(gw_gu.reshape(groups_z, dim // groups_z, -1), 0)
    z_down = z_half_send(gw_down[:ff_own].reshape(groups_z, ff_blk, dim), 0)

    gg_mlp = jnp.sum(grad_norm2 * hidden1 * inv2, axis=0)
    grad_hidden = cot_own.astype(F32) + norm_back(grad_norm2, hidden1, inv2, norm_mlp)
    gh_own = grad_hidden.astype(BF)
    gh_two = pair_rows(gh_own, swap_of(gh_own, 1, 0))
    wo_rows = lax.dynamic_slice_in_dim(wo, half_dim * core, half_dim, 0)
    grad_att = dot(gh_two, wo_rows, 1, 1, BF)

    rope_t = jnp.stack([jnp.cos(angles).T, jnp.sin(angles).T])
    gq_bf, gq_sum, dkvs = attention_bwd(idx, q_scaled, grad_att, att_heads, lse, rope_t, kvs)
    dkv_recv = [dkvs[0]] + [swap_of(dkvs[k], 2 * k, 0) for k in range(1, pairs)]

    xc = jnp.stack([wt, core]).astype(jnp.int32)
    oq_mine, oq_send = outer_terms(xc, att_two, gh_two, normed1_bf, gq_bf, ctx_count)
    gn1_q = dot(gq_bf, wq[:, :head_cols], 1, 1)

    rows = dim // device_count

    def plane_step(a, bit, cx, wx):
        return pick(a, bit), swap_of(pick(a, 1 - bit), cx, wx)

    oq_recv = swap_of(oq_send, 0, 1)
    z_down, _ = z_half_more(z_down, gh_own)
    z_gu, _ = z_half_more(z_gu, oq_send)
    out_quad = plane_quad(out_keep, out_send)
    out_recv = plane_sends(out_quad)

    dkv = dkv_recv[0].astype(F32)
    for v in dkv_recv[1:]:
        dkv = dkv + v.astype(F32)
    gkv = jnp.concatenate([unrope(dkv[:, :HD]), dkv[:, HD:]], axis=1)
    gkv_bf = gkv.astype(BF)
    gn1_part = gn1_q + dot(gkv_bf, wq[:, head_cols:], 1, 1)
    gn1_swap = swap_of(peer_rows(gn1_part), 1, 0)
    gw_kv = dot(normed1_bf, gkv_bf, 0, 0, BF)
    gb = jnp.concatenate([gq_sum[0], jnp.sum(gkv, axis=0)])
    grad_norm1 = own_rows(gn1_part) + gn1_swap
    x32 = x_own.astype(F32)
    inv1_own = own_rows(inv1)
    gg_attn = jnp.sum(grad_norm1 * x32 * inv1_own, axis=0)

    zero_q = jnp.zeros((head_cols,), F32)
    zero_h = jnp.zeros((HD,), F32)
    gb_full = jnp.concatenate(
        [
            by_bit(core, gb[:head_cols], zero_q, 0),
            by_bit(core, gb[head_cols:rope_cols], zero_h, 0),
            by_bit(core, gb[rope_cols:], zero_h, 0),
        ]
    )
    split_at = dim + kv_cols
    n_qk = split_at // device_count
    n_v = kv_cols // device_count
    small = jnp.concatenate(
        [
            gg_attn.reshape(device_count, rows),
            gg_mlp.reshape(device_count, rows),
            gb_full[:split_at].reshape(device_count, n_qk),
            gb_full[split_at:].reshape(device_count, n_v),
        ],
        axis=1,
    )
    n_small = small.shape[1]
    small = jnp.pad(small, ((0, 0), (0, 2 * HD - n_small)))
    tail = jnp.concatenate(
        [gw_kv.reshape(device_count, rows, 2 * HD), small.astype(BF)[:, None, :]], axis=1
    )
    tail_src = tail
    tail = tail.reshape(groups_z, 2, 2, 2, rows + 1, 2 * HD)
    tail = jnp.moveaxis(tail, (1, 3), (0, 1))
    kv_mine, kv_recv = plane_step(tail, chip_y, 2, 0)
    oq = (oq_mine.astype(F32) + gate(oq_recv, tail_src).astype(F32)).astype(BF)
    oq = jnp.moveaxis(oq.reshape(groups_z, 2, 2 * rows, 2 * head_cols), 1, 0)
    oq_mine, oq_recv = plane_step(oq, chip_y, 2, 0)
    tail = (kv_mine.astype(F32) + kv_recv.astype(F32)).astype(BF)
    kv_mine, kv_recv = plane_step(tail, wt, 0, 1)
    last = jnp.concatenate(
        [
            jnp.pad(
                (oq_mine.astype(F32) + gate(oq_recv, kv_mine).astype(F32)).reshape(
                    groups_z, 2, rows, 2 * head_cols
                ),
                ((0, 0), (0, 0), (0, 1), (0, 0)),
            ),
            kv_mine.astype(F32) + kv_recv.astype(F32),
        ],
        axis=-1,
    ).astype(BF)
    sum_gu = z_half_last(z_gu, last).astype(BF)
    sum_gu = sum_gu.reshape(8, rows, 2 * ff_wide)
    parts = [pick(sum_gu, plane)] + [
        swap_of(pick(sum_gu, plane ^ k), k >> 1, k & 1) for k in range(1, 8)
    ]
    last = last.reshape(ctx_count // 2, rows + 1, -1)
    last_all = lax.all_to_all(last, ("group", "core"), 0, 0, tiled=True)
    output = (hidden1 + plane_finish(out_quad, [gate(out_recv[0], last)] + out_recv[1:])).astype(BF)
    grad_input = grad_hidden + norm_back(after(grad_norm1, last), x32, inv1_own, norm_attn)
    shard_down = z_half_last(z_down, last) * factor
    last_all = last_all.reshape(groups_z, 2, rows + 1, -1).astype(F32)
    last_sum = jnp.sum(last_all, axis=0) * factor
    sum_oq, tail = last_sum[:, :rows, : 2 * head_cols], last_sum[:, :, 2 * head_cols :]
    shard_gate, shard_up = assemble(plane[None].astype(jnp.int32), parts, groups_z, ff_blk, ff_wide, factor)

    shard_wout = jnp.concatenate([sum_oq[0, :, :head_cols], sum_oq[1, :, :head_cols]], axis=1)
    low, high = tail[0], tail[1]
    shard_qkv = jnp.concatenate(
        [
            sum_oq[0, :, head_cols:],
            sum_oq[1, :, head_cols:],
            low[:rows, :HD],
            high[:rows, :HD],
            low[:rows, HD:],
            high[:rows, HD:],
        ],
        axis=1,
    )
    vec = low[rows, :n_small] + high[rows, :n_small]
    return (
        output[None],
        grad_input[None],
        vec[:rows],
        shard_qkv,
        vec[2 * rows : 2 * rows + n_qk],
        vec[2 * rows + n_qk :],
        shard_wout,
        vec[rows : 2 * rows],
        shard_gate,
        shard_up,
        shard_down,
    )


def solution(mesh):
    ctx_count, wt_count = mesh.devices.shape
    split = Mesh(mesh.devices.reshape(ctx_count // 4, 2, 2, wt_count), CTX + ("wt",))
    both = P(CTX + ("wt",))
    both_rows = P(CTX + ("wt",), None)
    tokens = P("wt", CTX, None)
    weight = P("wt", None)

    return jax.shard_map(
        shards,
        mesh=split,
        in_specs=(tokens, tokens, P(), weight, P(), weight, P(), weight, weight, weight),
        out_specs=(tokens, tokens, both, both_rows, both, both)
        + (both_rows, both, both_rows, both_rows, both_rows),
        check_vma=False,
    )
```

profile of v0, /device:TPU:0, one launch (start us, length us, event | category | flops | bytes accessed | tf_op | source)
XLA Modules:
  0.0 290.4 jit_solution(17351708853777144002)
XLA Ops:
  4.5 2.6 collective-permute-start.1
  11.4 9.9 %collective-permute-done.1 = bf16[448,576]{1,0:T(8,128)(2,1)} collective-permute-done((bf16[448,576]{1,0:T(8,128)(2,1)}, bf16[448,576]{1,0:T(8,128)(2,1)}, u32[]{:S(2)}, u32[]{:S(2)}) %collective-permute-start.1) | collective-permute-done | bytes 516128 | tf_op jit(solution)/shard_map/ppermute | solution.py:557
  21.3 1.7 maximum_select_fusion.1
  24.5 2.1 collective-permute-start.2
  26.6 1.6 collective-permute-start.3
  28.7 3.0 %collective-permute-start.5 = (bf16[256,128]{1,0:T(8,128)(2,1)S(1)}, bf16[256,128]{1,0:T(8,128)(2,1)S(1)}, u32[]{:S(2)}, u32[]{:S(2)}) collective-permute-start(bf16[256,128]{1,0:T(8,128)(2,1)S(1)} %pad_maximum_fusion.9.refs_0_), channel_id=1, source_target_pairs={{0,16},{2,18},{4,20},{6,22},{8,24},{10,26},{12,28},{14,30},{16,0},... | collective-permute-start | bytes 196616 | tf_op jit(solution)/shard_map/ppermute | solution.py:555
  31.7 1.8 collective-permute-start.6
  33.6 3.0 %collective-permute-start.7 = (bf16[256,128]{1,0:T(8,128)(2,1)S(1)}, bf16[256,128]{1,0:T(8,128)(2,1)S(1)}, u32[]{:S(2)}, u32[]{:S(2)}) collective-permute-start(bf16[256,128]{1,0:T(8,128)(2,1)S(1)} %pad_maximum_fusion.9.refs_0_), channel_id=1, source_target_pairs={{0,24},{2,26},{4,28},{6,30},{8,16},{10,18},{12,20},{14,22},{16,8},... | collective-permute-start | bytes 196616 | tf_op jit(solution)/shard_map/ppermute | solution.py:555
  37.5 1.5 collective-permute-start.19
  39.0 2.9 collective-permute-done.6.refs_5_
  42.1 2.4 collective-permute-start.21
  45.2 10.7 %attn_fwd.1 = (bf16[256,448]{1,0:T(8,128)(2,1)}, f32[2,1,896]{2,1,0:T(1,128)}) custom-call(s32[2]{0:T(128)} %pad_add_fusion.idx_ref, bf16[256,448]{1,0:T(8,128)(2,1)} %slice_multiply_fusion.1.q_ref, bf16[256,128]{1,0:T(8,128)(2,1)} %copy-done.20, bf16[256,128]{1,0:T(8,128)(2,1)} %copy-done.21, bf16[256,128]{1,0:T(8,128)(2,1)} %copy-done.22, ...), custom_call_target="tpu_custom_call" | custom-call | tf_op jit(solution)/shard_map/attn_fwd/pallas_call | solution.py:290
  56.6 4.8 %hidden_columns.3 = bf16[224,1280]{1,0:T(8,128)(2,1)} custom-call(s32[2]{0:T(128)} %pad_add_fusion.2.idx_ref, bf16[448,4864]{1,0:T(8,128)(2,1)} %gate_ref.1, bf16[448,4864]{1,0:T(8,128)(2,1)} %up_ref.1), custom_call_target="tpu_custom_call" | custom-call | tf_op jit(solution)/shard_map/hidden_columns/pallas_call | solution.py:382
  66.5 1.7 maximum_select_fusion.2
  71.4 13.0 %collective-permute-done.28.refs_20_ = bf16[152,896]{1,0:T(8,128)(2,1)} collective-permute-done((bf16[152,896]{1,0:T(8,128)(2,1)S(1)}, bf16[152,896]{1,0:T(8,128)(2,1)}, u32[]{:S(2)}, u32[]{:S(2)}) %collective-permute-start.28) | collective-permute-done | bytes 272416 | tf_op jit(solution)/shard_map/ppermute | solution.py:557
  85.0 1.9 collective-permute-start.14
  89.8 6.6 %collective-permute-done.13.refs_2_ = bf16[128,896]{1,0:T(8,128)(2,1)} collective-permute-done((bf16[128,896]{1,0:T(8,128)(2,1)}, bf16[128,896]{1,0:T(8,128)(2,1)}, u32[]{:S(2)}, u32[]{:S(2)}) %collective-permute-start.13) | collective-permute-done | bytes 229408 | tf_op jit(solution)/shard_map/ppermute | solution.py:555
  97.5 1.9 constant_dynamic-slice_fusion.2
  99.4 5.9 %hidden_columns.2.refs_16_ = bf16[448,1280]{1,0:T(8,128)(2,1)} custom-call(s32[2]{0:T(128)} %pad_add_fusion.1.idx_ref, bf16[448,4864]{1,0:T(8,128)(2,1)} %gate_ref.1, bf16[448,4864]{1,0:T(8,128)(2,1)} %up_ref.1), custom_call_target="tpu_custom_call" | custom-call | tf_op jit(solution)/shard_map/hidden_columns/pallas_call | solution.py:382
  108.1 14.1 %mlp.1 = (f32[512,896]{1,0:T(8,128)}, bf16[512,896]{1,0:T(8,128)(2,1)}, bf16[1024,1280]{1,0:T(8,128)(2,1)}, bf16[1024,640]{1,0:T(8,128)(2,1)}, bf16[1024,896]{1,...) custom-call(s32[2]{0:T(128)} %pad_add_fusion.4.idx_ref, ...), custom_call_target="tpu_custom_call" | custom-call | tf_op jit(solution)/shard_map/mlp/pallas_call | solution.py:457
  122.6 2.5 fusion.8
  127.9 1.5 collective-permute-start.34
  130.5 1.6 fusion.81
  134.2 2.9 fusion.80
  141.8 1.8 fusion.62
  147.6 11.7 %attn_bwd.1 = (bf16[256,448]{1,0:T(8,128)(2,1)}, f32[1,448]{1,0:T(1,128)}, bf16[256,128]{1,0:T(8,128)(2,1)}, bf16[256,128]{1,0:T(8,128)(2,1)}, bf16[256,128]{1,0...) custom-call(s32[2]{0:T(128)} %pad_add_fusion.idx_ref, ...), custom_call_target="tpu_custom_call" | custom-call | tf_op jit(solution)/shard_map/attn_bwd/pallas_call | solution.py:315
  159.3 4.1 %collective-permute-start.44 = (bf16[256,128]{1,0:T(8,128)(2,1)}, bf16[256,128]{1,0:T(8,128)(2,1)S(1)}, u32[]{:S(2)}, u32[]{:S(2)}) collective-permute-start(bf16[256,128]{1,0:T(8,128)(2,1)} %get-tuple-element.88), channel_id=1, source_target_pairs={{0,28},{2,30},{4,24},{6,26},{8,20},{10,22},{12,16},{14,18},{16,12}... | collective-permute-start | bytes 196616 | tf_op jit(solution)/shard_map/ppermute | solution.py:555
  164.1 3.1 %collective-permute-start.41 = (bf16[256,128]{1,0:T(8,128)(2,1)}, bf16[256,128]{1,0:T(8,128)(2,1)S(1)}, u32[]{:S(2)}, u32[]{:S(2)}) collective-permute-start(bf16[256,128]{1,0:T(8,128)(2,1)} %get-tuple-element.85), channel_id=1, source_target_pairs={{0,16},{2,18},{4,20},{6,22},{8,24},{10,26},{12,28},{14,30},{16,0},... | collective-permute-start | bytes 196616 | tf_op jit(solution)/shard_map/ppermute | solution.py:555
  169.5 3.7 %outer_terms.1 = (bf16[8,56,896]{2,1,0:T(8,128)(2,1)}, bf16[8,56,896]{2,1,0:T(8,128)(2,1)}) custom-call(s32[2]{0:T(128)} %pad_add_fusion.3.idx_ref, bf16[256,896]{1,0:T(8,128)(2,1)} %copy-done.8, bf16[256,896]{1,0:T(8,128)(2,1)} %pad_maximum_fusion.4.gh_ref, bf16[256,896]{1,0:T(8,128)(2,1)} %copy-done, bf16[256,448]{1,0:T(8,128)(2,1)} %get-tuple-element.78.gq_ref), custom_call_target="tpu_custom_call" | custom-call | tf_op jit(solution)/shard_map/outer_terms/pallas_call | solution.py:496
  176.1 1.5 collective-permute-start.49
  180.3 1.9 collective-permute-done.38
  187.5 3.9 %collective-permute-done.60 = bf16[2,152,896]{2,1,0:T(8,128)(2,1)} collective-permute-done((bf16[2,152,896]{2,1,0:T(8,128)(2,1)}, bf16[2,152,896]{2,1,0:T(8,128)(2,1)}, u32[]{:S(2)}, u32[]{:S(2)}) %collective-permute-start.60) | collective-permute-done | bytes 544800 | tf_op jit(solution)/shard_map/ppermute | solution.py:719
  196.4 3.7 %collective-permute-done.47 = bf16[2,4,2,29,128]{4,3,0,2,1:T(8,128)(2,1)S(1)} collective-permute-done((bf16[2,4,2,29,128]{4,3,0,2,1:T(8,128)(2,1)S(1)}, bf16[2,4,2,29,128]{4,3,0,2,1:T(8,128)(2,1)S(1)}, u32[]{:S(2)}, u32[]{:S(2)}) %collective-permute-start.47) | collective-permute-done | bytes 118816 | tf_op jit(solution)/shard_map/ppermute | solution.py:555
  201.0 14.7 %collective-permute-done.51 = bf16[2,224,1280]{2,1,0:T(8,128)(2,1)} collective-permute-done((bf16[2,224,1280]{2,1,0:T(8,128)(2,1)}, bf16[2,224,1280]{2,1,0:T(8,128)(2,1)}, u32[]{:S(2)}, u32[]{:S(2)}) %collective-permute-start.51) | collective-permute-done | bytes 1146912 | tf_op jit(solution)/shard_map/ppermute | solution.py:719
  216.2 1.9 fusion
  219.0 1.6 add_convert_fusion
  220.6 1.6 collective-permute-start.46
  223.1 1.6 collective-permute-start.61
  225.3 3.3 %collective-permute-done.46.value_ref = bf16[4,56,896]{2,1,0:T(8,128)(2,1)} collective-permute-done((bf16[4,56,896]{2,1,0:T(8,128)(2,1)S(1)}, bf16[4,56,896]{2,1,0:T(8,128)(2,1)}, u32[]{:S(2)}, u32[]{:S(2)}) %collective-permute-start.46) | collective-permute-done | bytes 401440 | tf_op jit(solution)/shard_map/ppermute | solution.py:555
  228.6 2.4 collective-permute-start.52
  233.3 3.7 %all-to-all-start = ((bf16[8,29,1024]{2,1,0:T(8,128)(2,1)}), bf16[8,29,1024]{2,1,0:T(8,128)(2,1)S(1)}, u32[]{:S(2)}, u32[]{:S(2)}) async-start(bf16[8,29,1024]{2,1,0:T(8,128)(2,1)} %pad_maximum_fusion.1.done_ref), calls=%async_computation | async-start | bytes 1048576 | tf_op jit(solution)/shard_map/all_to_all | solution.py:833
  238.1 28.7 %collective-permute-done.52.value_ref = bf16[1,224,1280]{2,1,0:T(8,128)(2,1)} collective-permute-done((bf16[1,224,1280]{2,1,0:T(8,128)(2,1)}, bf16[1,224,1280]{2,1,0:T(8,128)(2,1)}, u32[]{:S(2)}, u32[]{:S(2)}) %collective-permute-start.52) | collective-permute-done | bytes 573472 | tf_op jit(solution)/shard_map/ppermute | solution.py:719
  269.7 2.6 fusion.23
  274.1 1.8 collective-permute-start.57
  276.1 2.2 collective-permute-start.59
  278.3 1.8 multiply_bitcast_fusion
  281.1 1.9 collective-permute-done.58.refs_6_
  283.7 2.8 assemble.1
  (315 shorter events, 78.6 us)
Async XLA Ops:
  0.7 10.3 %collective-permute-start = (bf16[128,896]{1,0:T(8,128)(2,1)}, bf16[128,896]{1,0:T(8,128)(2,1)S(1)}, u32[]{:S(2)}, u32[]{:S(2)}) collective-permute-start(bf16[128,896]{1,0:T(8,128)(2,1)} %bitcast.140), channel_id=1, source_target_pairs={{0,2},{2,0},{4,6},{6,4},{8,10},{10,8},{12,14},{14,12},{16,18},{18,... | collective-permute-start | bytes 688136 | tf_op jit(solution)/shard_map/ppermute | solution.py:555
  4.5 16.7 %collective-permute-start.1 = (bf16[448,576]{1,0:T(8,128)(2,1)}, bf16[448,576]{1,0:T(8,128)(2,1)}, u32[]{:S(2)}, u32[]{:S(2)}) collective-permute-start(bf16[448,576]{1,0:T(8,128)(2,1)} %pad_maximum_fusion), channel_id=1, source_target_pairs={{0,1},{1,0},{2,3},{3,2},{4,5},{5,4},{6,7},{7,6},{8,9},{9,8},{10,11... | collective-permute-start | bytes 1548296 | tf_op jit(solution)/shard_map/ppermute | solution.py:557
  8.1 54.3 %collective-permute-start.10 = (bf16[448,448]{1,0:T(8,128)(2,1)}, bf16[448,448]{1,0:T(8,128)(2,1)}, u32[]{:S(2)}, u32[]{:S(2)}) collective-permute-start(bf16[448,448]{1,0:T(8,128)(2,1)} %constant_dynamic-slice_fusion.3), channel_id=1, source_target_pairs={{0,1},{1,0},{2,3},{3,2},{4,5},{5,4},{6,7},{7,6},{8,9},{9,8},{10,11... | collective-permute-start | bytes 1204232 | tf_op jit(solution)/shard_map/ppermute | solution.py:557
  24.5 7.3 %collective-permute-start.2 = (bf16[256,128]{1,0:T(8,128)(2,1)S(1)}, bf16[256,128]{1,0:T(8,128)(2,1)S(1)}, u32[]{:S(2)}, u32[]{:S(2)}) collective-permute-start(bf16[256,128]{1,0:T(8,128)(2,1)S(1)} %pad_maximum_fusion.9.refs_0_), channel_id=1, source_target_pairs={{0,4},{2,6},{4,0},{6,2},{8,12},{10,14},{12,8},{14,10},{16,20},{18,... | collective-permute-start | bytes 196616 | tf_op jit(solution)/shard_map/ppermute | solution.py:555
  28.2 8.5 %collective-permute-start.4 = (bf16[256,128]{1,0:T(8,128)(2,1)S(1)}, bf16[256,128]{1,0:T(8,128)(2,1)S(1)}, u32[]{:S(2)}, u32[]{:S(2)}) collective-permute-start(bf16[256,128]{1,0:T(8,128)(2,1)S(1)} %pad_maximum_fusion.9.refs_0_), channel_id=1, source_target_pairs={{0,12},{2,14},{4,8},{6,10},{8,4},{10,6},{12,0},{14,2},{16,28},{18,... | collective-permute-start | bytes 196616 | tf_op jit(solution)/shard_map/ppermute | solution.py:555
  28.7 8.8 %collective-permute-start.5 = (bf16[256,128]{1,0:T(8,128)(2,1)S(1)}, bf16[256,128]{1,0:T(8,128)(2,1)S(1)}, u32[]{:S(2)}, u32[]{:S(2)}) collective-permute-start(bf16[256,128]{1,0:T(8,128)(2,1)S(1)} %pad_maximum_fusion.9.refs_0_), channel_id=1, source_target_pairs={{0,16},{2,18},{4,20},{6,22},{8,24},{10,26},{12,28},{14,30},{16,0},... | collective-permute-start | bytes 196616 | tf_op jit(solution)/shard_map/ppermute | solution.py:555
  31.7 10.2 %collective-permute-start.6 = (bf16[256,128]{1,0:T(8,128)(2,1)S(1)}, bf16[256,128]{1,0:T(8,128)(2,1)S(1)}, u32[]{:S(2)}, u32[]{:S(2)}) collective-permute-start(bf16[256,128]{1,0:T(8,128)(2,1)S(1)} %pad_maximum_fusion.9.refs_0_), channel_id=1, source_target_pairs={{0,20},{2,22},{4,16},{6,18},{8,28},{10,30},{12,24},{14,26},{16,4},... | collective-permute-start | bytes 196616 | tf_op jit(solution)/shard_map/ppermute | solution.py:555
  33.6 8.5 %collective-permute-start.7 = (bf16[256,128]{1,0:T(8,128)(2,1)S(1)}, bf16[256,128]{1,0:T(8,128)(2,1)S(1)}, u32[]{:S(2)}, u32[]{:S(2)}) collective-permute-start(bf16[256,128]{1,0:T(8,128)(2,1)S(1)} %pad_maximum_fusion.9.refs_0_), channel_id=1, source_target_pairs={{0,24},{2,26},{4,28},{6,30},{8,16},{10,18},{12,20},{14,22},{16,8},... | collective-permute-start | bytes 196616 | tf_op jit(solution)/shard_map/ppermute | solution.py:555
  36.6 7.9 %collective-permute-start.8 = (bf16[256,128]{1,0:T(8,128)(2,1)S(1)}, bf16[256,128]{1,0:T(8,128)(2,1)S(1)}, u32[]{:S(2)}, u32[]{:S(2)}) collective-permute-start(bf16[256,128]{1,0:T(8,128)(2,1)S(1)} %pad_maximum_fusion.9.refs_0_), channel_id=1, source_target_pairs={{0,28},{2,30},{4,24},{6,26},{8,20},{10,22},{12,16},{14,18},{16,12}... | collective-permute-start | bytes 196616 | tf_op jit(solution)/shard_map/ppermute | solution.py:555
  37.5 32.8 %collective-permute-start.19 = (bf16[128,896]{1,0:T(8,128)(2,1)}, bf16[128,896]{1,0:T(8,128)(2,1)}, u32[]{:S(2)}, u32[]{:S(2)}) collective-permute-start(bf16[128,896]{1,0:T(8,128)(2,1)} %bitcast.12.refs_8_), channel_id=1, source_target_pairs={{0,1},{1,0},{2,3},{3,2},{4,5},{5,4},{6,7},{7,6},{8,9},{9,8},{10,11... | collective-permute-start | bytes 688136 | tf_op jit(solution)/shard_map/ppermute | solution.py:557
  41.9 28.5 %collective-permute-start.20 = (bf16[128,896]{1,0:T(8,128)(2,1)}, bf16[128,896]{1,0:T(8,128)(2,1)}, u32[]{:S(2)}, u32[]{:S(2)}) collective-permute-start(bf16[128,896]{1,0:T(8,128)(2,1)} %bitcast.12.refs_8_), channel_id=1, source_target_pairs={{0,4},{2,6},{4,0},{6,2},{8,12},{10,14},{12,8},{14,10},{16,20},{18,... | collective-permute-start | bytes 688136 | tf_op jit(solution)/shard_map/ppermute | solution.py:555
  42.1 45.0 %collective-permute-start.21 = (bf16[128,896]{1,0:T(8,128)(2,1)}, bf16[128,896]{1,0:T(8,128)(2,1)}, u32[]{:S(2)}, u32[]{:S(2)}) collective-permute-start(bf16[128,896]{1,0:T(8,128)(2,1)} %bitcast.12.refs_8_), channel_id=1, source_target_pairs={{0,5},{1,4},{2,7},{3,6},{4,1},{5,0},{6,3},{7,2},{8,13},{9,12},{10,... | collective-permute-start | bytes 688136 | tf_op jit(solution)/shard_map/ppermute | solution.py:558
  55.9 7.5 %collective-permute-start.9 = (bf16[256,448]{1,0:T(8,128)(2,1)}, bf16[256,448]{1,0:T(8,128)(2,1)S(1)}, u32[]{:S(2)}, u32[]{:S(2)}) collective-permute-start(bf16[256,448]{1,0:T(8,128)(2,1)} %get-tuple-element.53.att_ref), channel_id=1, source_target_pairs={{0,2},{2,0},{4,6},{6,4},{8,10},{10,8},{12,14},{14,12},{16,18},{18,... | collective-permute-start | bytes 688136 | tf_op jit(solution)/shard_map/ppermute | solution.py:555
  62.4 22.6 %collective-permute-start.26 = (bf16[224,1280]{1,0:T(8,128)(2,1)}, bf16[224,1280]{1,0:T(8,128)(2,1)}, u32[]{:S(2)}, u32[]{:S(2)}) collective-permute-start(bf16[224,1280]{1,0:T(8,128)(2,1)} %hidden_columns.3), channel_id=1, source_target_pairs={{0,1},{1,0},{2,3},{3,2},{4,5},{5,4},{6,7},{7,6},{8,9},{9,8},{10,11... | collective-permute-start | bytes 1720328 | tf_op jit(solution)/shard_map/ppermute | solution.py:557
  65.4 19.0 %collective-permute-start.28 = (bf16[152,896]{1,0:T(8,128)(2,1)S(1)}, bf16[152,896]{1,0:T(8,128)(2,1)}, u32[]{:S(2)}, u32[]{:S(2)}) collective-permute-start(bf16[152,896]{1,0:T(8,128)(2,1)S(1)} %dynamic-slice_bitcast_fusion.3), channel_id=1, source_target_pairs={{0,1},{1,0},{2,3},{3,2},{4,5},{5,4},{6,7},{7,6},{8,9},{9,8},{10,11... | collective-permute-start | bytes 817160 | tf_op jit(solution)/shard_map/ppermute | solution.py:557
  70.4 17.3 %collective-permute-start.22 = (bf16[128,896]{1,0:T(8,128)(2,1)}, bf16[128,896]{1,0:T(8,128)(2,1)}, u32[]{:S(2)}, u32[]{:S(2)}) collective-permute-start(bf16[128,896]{1,0:T(8,128)(2,1)} %bitcast.12.refs_8_), channel_id=1, source_target_pairs={{0,2},{2,0},{4,6},{6,4},{8,10},{10,8},{12,14},{14,12},{16,18},{18,... | collective-permute-start | bytes 688136 | tf_op jit(solution)/shard_map/ppermute | solution.py:555
  70.4 19.4 %collective-permute-start.12 = (bf16[128,896]{1,0:T(8,128)(2,1)}, bf16[128,896]{1,0:T(8,128)(2,1)}, u32[]{:S(2)}, u32[]{:S(2)}) collective-permute-start(bf16[128,896]{1,0:T(8,128)(2,1)} %multiply_convert_fusion.refs_0_), channel_id=1, source_target_pairs={{0,1},{1,0},{2,3},{3,2},{4,5},{5,4},{6,7},{7,6},{8,9},{9,8},{10,11... | collective-permute-start | bytes 688136 | tf_op jit(solution)/shard_map/ppermute | solution.py:557
  84.4 11.9 %collective-permute-start.13 = (bf16[128,896]{1,0:T(8,128)(2,1)}, bf16[128,896]{1,0:T(8,128)(2,1)}, u32[]{:S(2)}, u32[]{:S(2)}) collective-permute-start(bf16[128,896]{1,0:T(8,128)(2,1)} %multiply_convert_fusion.refs_0_), channel_id=1, source_target_pairs={{0,4},{2,6},{4,0},{6,2},{8,12},{10,14},{12,8},{14,10},{16,20},{18,... | collective-permute-start | bytes 688136 | tf_op jit(solution)/shard_map/ppermute | solution.py:555
  85.0 11.4 %collective-permute-start.14 = (bf16[128,896]{1,0:T(8,128)(2,1)}, bf16[128,896]{1,0:T(8,128)(2,1)}, u32[]{:S(2)}, u32[]{:S(2)}) collective-permute-start(bf16[128,896]{1,0:T(8,128)(2,1)} %multiply_convert_fusion.refs_0_), channel_id=1, source_target_pairs={{0,5},{1,4},{2,7},{3,6},{4,1},{5,0},{6,3},{7,2},{8,13},{9,12},{10,... | collective-permute-start | bytes 688136 | tf_op jit(solution)/shard_map/ppermute | solution.py:558
  87.1 18.8 %collective-permute-start.29 = (bf16[152,896]{1,0:T(8,128)(2,1)}, bf16[152,896]{1,0:T(8,128)(2,1)}, u32[]{:S(2)}, u32[]{:S(2)}) collective-permute-start(bf16[152,896]{1,0:T(8,128)(2,1)} %collective-permute-done.28.refs_20_), channel_id=1, source_target_pairs={{0,8},{2,10},{4,12},{6,14},{8,0},{10,2},{12,4},{14,6},{16,24},{18,... | collective-permute-start | bytes 817160 | tf_op jit(solution)/shard_map/ppermute | solution.py:637
  87.7 20.4 %collective-permute-start.27 = (bf16[224,1280]{1,0:T(8,128)(2,1)}, bf16[224,1280]{1,0:T(8,128)(2,1)}, u32[]{:S(2)}, u32[]{:S(2)}) collective-permute-start(bf16[224,1280]{1,0:T(8,128)(2,1)} %collective-permute-done.26.refs_17_), channel_id=1, source_target_pairs={{0,8},{2,10},{4,12},{6,14},{8,0},{10,2},{12,4},{14,6},{16,24},{18,... | collective-permute-start | bytes 1720328 | tf_op jit(solution)/shard_map/ppermute | solution.py:637
  89.8 15.5 %collective-permute-start.23 = (bf16[128,896]{1,0:T(8,128)(2,1)}, bf16[128,896]{1,0:T(8,128)(2,1)}, u32[]{:S(2)}, u32[]{:S(2)}) collective-permute-start(bf16[128,896]{1,0:T(8,128)(2,1)} %collective-permute-done.19.refs_9_), channel_id=1, source_target_pairs={{0,2},{2,0},{4,6},{6,4},{8,10},{10,8},{12,14},{14,12},{16,18},{18,... | collective-permute-start | bytes 688136 | tf_op jit(solution)/shard_map/ppermute | solution.py:555
  96.4 9.0 %collective-permute-start.24 = (bf16[128,896]{1,0:T(8,128)(2,1)}, bf16[128,896]{1,0:T(8,128)(2,1)}, u32[]{:S(2)}, u32[]{:S(2)}) collective-permute-start(bf16[128,896]{1,0:T(8,128)(2,1)} %collective-permute-done.20.refs_10_), channel_id=1, source_target_pairs={{0,2},{2,0},{4,6},{6,4},{8,10},{10,8},{12,14},{14,12},{16,18},{18,... | collective-permute-start | bytes 688136 | tf_op jit(solution)/shard_map/ppermute | solution.py:555
  96.4 9.5 %collective-permute-start.25 = (bf16[128,896]{1,0:T(8,128)(2,1)}, bf16[128,896]{1,0:T(8,128)(2,1)}, u32[]{:S(2)}, u32[]{:S(2)}) collective-permute-start(bf16[128,896]{1,0:T(8,128)(2,1)} %collective-permute-done.21.refs_11_), channel_id=1, source_target_pairs={{0,2},{2,0},{4,6},{6,4},{8,10},{10,8},{12,14},{14,12},{16,18},{18,... | collective-permute-start | bytes 688136 | tf_op jit(solution)/shard_map/ppermute | solution.py:555
  125.2 13.2 %collective-permute-start.30 = (bf16[512,896]{1,0:T(8,128)(2,1)S(1)}, bf16[512,896]{1,0:T(8,128)(2,1)S(1)}, u32[]{:S(2)}, u32[]{:S(2)}) collective-permute-start(bf16[512,896]{1,0:T(8,128)(2,1)S(1)} %fusion.8), channel_id=1, source_target_pairs={{0,2},{2,0},{4,6},{6,4},{8,10},{10,8},{12,14},{14,12},{16,18},{18,... | collective-permute-start | bytes 2752520 | tf_op jit(solution)/shard_map/ppermute | solution.py:555
  126.9 13.8 %collective-permute-start.35 = (bf16[128,896]{1,0:T(8,128)(2,1)S(1)}, bf16[128,896]{1,0:T(8,128)(2,1)S(1)}, u32[]{:S(2)}, u32[]{:S(2)}) collective-permute-start(bf16[128,896]{1,0:T(8,128)(2,1)S(1)} %get-tuple-element.113), channel_id=1, source_target_pairs={{0,5},{1,4},{2,7},{3,6},{4,1},{5,0},{6,3},{7,2},{8,13},{9,12},{10,... | collective-permute-start | bytes 688136 | tf_op jit(solution)/shard_map/ppermute | solution.py:558
  127.9 12.8 %collective-permute-start.34 = (bf16[128,896]{1,0:T(8,128)(2,1)S(1)}, bf16[128,896]{1,0:T(8,128)(2,1)S(1)}, u32[]{:S(2)}, u32[]{:S(2)}) collective-permute-start(bf16[128,896]{1,0:T(8,128)(2,1)S(1)} %get-tuple-element.114), channel_id=1, source_target_pairs={{0,4},{2,6},{4,0},{6,2},{8,12},{10,14},{12,8},{14,10},{16,20},{18,... | collective-permute-start | bytes 688136 | tf_op jit(solution)/shard_map/ppermute | solution.py:555
  129.4 11.3 %collective-permute-start.33 = (bf16[128,896]{1,0:T(8,128)(2,1)S(1)}, bf16[128,896]{1,0:T(8,128)(2,1)S(1)}, u32[]{:S(2)}, u32[]{:S(2)}) collective-permute-start(bf16[128,896]{1,0:T(8,128)(2,1)S(1)} %get-tuple-element.112), channel_id=1, source_target_pairs={{0,1},{1,0},{2,3},{3,2},{4,5},{5,4},{6,7},{7,6},{8,9},{9,8},{10,11... | collective-permute-start | bytes 688136 | tf_op jit(solution)/shard_map/ppermute | solution.py:557
  159.3 13.9 %collective-permute-start.44 = (bf16[256,128]{1,0:T(8,128)(2,1)}, bf16[256,128]{1,0:T(8,128)(2,1)S(1)}, u32[]{:S(2)}, u32[]{:S(2)}) collective-permute-start(bf16[256,128]{1,0:T(8,128)(2,1)} %get-tuple-element.88), channel_id=1, source_target_pairs={{0,28},{2,30},{4,24},{6,26},{8,20},{10,22},{12,16},{14,18},{16,12}... | collective-permute-start | bytes 196616 | tf_op jit(solution)/shard_map/ppermute | solution.py:555
  163.4 10.5 %collective-permute-start.43 = (bf16[256,128]{1,0:T(8,128)(2,1)}, bf16[256,128]{1,0:T(8,128)(2,1)S(1)}, u32[]{:S(2)}, u32[]{:S(2)}) collective-permute-start(bf16[256,128]{1,0:T(8,128)(2,1)} %get-tuple-element.87), channel_id=1, source_target_pairs={{0,24},{2,26},{4,28},{6,30},{8,16},{10,18},{12,20},{14,22},{16,8},... | collective-permute-start | bytes 196616 | tf_op jit(solution)/shard_map/ppermute | solution.py:555
  163.4 11.9 %collective-permute-start.42 = (bf16[256,128]{1,0:T(8,128)(2,1)}, bf16[256,128]{1,0:T(8,128)(2,1)S(1)}, u32[]{:S(2)}, u32[]{:S(2)}) collective-permute-start(bf16[256,128]{1,0:T(8,128)(2,1)} %get-tuple-element.86), channel_id=1, source_target_pairs={{0,20},{2,22},{4,16},{6,18},{8,28},{10,30},{12,24},{14,26},{16,4},... | collective-permute-start | bytes 196616 | tf_op jit(solution)/shard_map/ppermute | solution.py:555
  164.1 12.0 %collective-permute-start.41 = (bf16[256,128]{1,0:T(8,128)(2,1)}, bf16[256,128]{1,0:T(8,128)(2,1)S(1)}, u32[]{:S(2)}, u32[]{:S(2)}) collective-permute-start(bf16[256,128]{1,0:T(8,128)(2,1)} %get-tuple-element.85), channel_id=1, source_target_pairs={{0,16},{2,18},{4,20},{6,22},{8,24},{10,26},{12,28},{14,30},{16,0},... | collective-permute-start | bytes 196616 | tf_op jit(solution)/shard_map/ppermute | solution.py:555
  167.2 10.4 %collective-permute-start.40 = (bf16[256,128]{1,0:T(8,128)(2,1)}, bf16[256,128]{1,0:T(8,128)(2,1)S(1)}, u32[]{:S(2)}, u32[]{:S(2)}) collective-permute-start(bf16[256,128]{1,0:T(8,128)(2,1)} %get-tuple-element.84), channel_id=1, source_target_pairs={{0,12},{2,14},{4,8},{6,10},{8,4},{10,6},{12,0},{14,2},{16,28},{18,... | collective-permute-start | bytes 196616 | tf_op jit(solution)/shard_map/ppermute | solution.py:555
  173.9 8.3 %collective-permute-start.38 = (bf16[256,128]{1,0:T(8,128)(2,1)S(1)}, bf16[256,128]{1,0:T(8,128)(2,1)S(1)}, u32[]{:S(2)}, u32[]{:S(2)}) collective-permute-start(bf16[256,128]{1,0:T(8,128)(2,1)S(1)} %copy-done.45), channel_id=1, source_target_pairs={{0,4},{2,6},{4,0},{6,2},{8,12},{10,14},{12,8},{14,10},{16,20},{18,... | collective-permute-start | bytes 196616 | tf_op jit(solution)/shard_map/ppermute | solution.py:555
  175.4 94.3 %collective-permute-start.50 = (bf16[128,896]{1,0:T(8,128)(2,1)}, bf16[128,896]{1,0:T(8,128)(2,1)}, u32[]{:S(2)}, u32[]{:S(2)}) collective-permute-start(bf16[128,896]{1,0:T(8,128)(2,1)} %get-tuple-element.116), channel_id=1, source_target_pairs={{0,5},{1,4},{2,7},{3,6},{4,1},{5,0},{6,3},{7,2},{8,13},{9,12},{10,... | collective-permute-start | bytes 688136 | tf_op jit(solution)/shard_map/ppermute | solution.py:558
  176.1 93.6 %collective-permute-start.49 = (bf16[128,896]{1,0:T(8,128)(2,1)}, bf16[128,896]{1,0:T(8,128)(2,1)}, u32[]{:S(2)}, u32[]{:S(2)}) collective-permute-start(bf16[128,896]{1,0:T(8,128)(2,1)} %get-tuple-element.117), channel_id=1, source_target_pairs={{0,4},{2,6},{4,0},{6,2},{8,12},{10,14},{12,8},{14,10},{16,20},{18,... | collective-permute-start | bytes 688136 | tf_op jit(solution)/shard_map/ppermute | solution.py:555
  177.6 59.5 %collective-permute-start.31 = (bf16[128,896]{1,0:T(8,128)(2,1)}, bf16[128,896]{1,0:T(8,128)(2,1)}, u32[]{:S(2)}, u32[]{:S(2)}) collective-permute-start(bf16[128,896]{1,0:T(8,128)(2,1)} %get-tuple-element.115), channel_id=1, source_target_pairs={{0,1},{1,0},{2,3},{3,2},{4,5},{5,4},{6,7},{7,6},{8,9},{9,8},{10,11... | collective-permute-start | bytes 688136 | tf_op jit(solution)/shard_map/ppermute | solution.py:557
  178.9 12.5 %collective-permute-start.60 = (bf16[2,152,896]{2,1,0:T(8,128)(2,1)}, bf16[2,152,896]{2,1,0:T(8,128)(2,1)}, u32[]{:S(2)}, u32[]{:S(2)}) collective-permute-start(bf16[2,152,896]{2,1,0:T(8,128)(2,1)} %dynamic-slice_bitcast_fusion.1), channel_id=1, source_target_pairs={{0,8},{2,10},{4,12},{6,14},{8,0},{10,2},{12,4},{14,6},{16,24},{18,... | collective-permute-start | bytes 1634312 | tf_op jit(solution)/shard_map/ppermute | solution.py:719
  186.8 7.8 %collective-permute-start.45 = (f32[128,896]{1,0:T(8,128)S(1)}, f32[128,896]{1,0:T(8,128)S(1)}, u32[]{:S(2)}, u32[]{:S(2)}) collective-permute-start(f32[128,896]{1,0:T(8,128)S(1)} %pad_maximum_fusion.5), channel_id=1, source_target_pairs={{0,2},{2,0},{4,6},{6,4},{8,10},{10,8},{12,14},{14,12},{16,18},{18,... | collective-permute-start | bytes 1376264 | tf_op jit(solution)/shard_map/ppermute | solution.py:555
  191.4 24.3 %collective-permute-start.51 = (bf16[2,224,1280]{2,1,0:T(8,128)(2,1)}, bf16[2,224,1280]{2,1,0:T(8,128)(2,1)}, u32[]{:S(2)}, u32[]{:S(2)}) collective-permute-start(bf16[2,224,1280]{2,1,0:T(8,128)(2,1)} %dynamic-slice_bitcast_fusion), channel_id=1, source_target_pairs={{0,8},{2,10},{4,12},{6,14},{8,0},{10,2},{12,4},{14,6},{16,24},{18,... | collective-permute-start | bytes 3440648 | tf_op jit(solution)/shard_map/ppermute | solution.py:719
  200.1 17.9 %collective-permute-start.37 = (bf16[8,56,896]{2,1,0:T(8,128)(2,1)}, bf16[8,56,896]{2,1,0:T(8,128)(2,1)S(1)}, u32[]{:S(2)}, u32[]{:S(2)}) collective-permute-start(bf16[8,56,896]{2,1,0:T(8,128)(2,1)} %get-tuple-element.80), channel_id=1, source_target_pairs={{0,1},{1,0},{2,3},{3,2},{4,5},{5,4},{6,7},{7,6},{8,9},{9,8},{10,11... | collective-permute-start | bytes 2408456 | tf_op jit(solution)/shard_map/ppermute | solution.py:557
  215.7 7.4 %collective-permute-start.48 = (bf16[4,2,29,128]{3,2,1,0:T(8,128)(2,1)S(1)}, bf16[4,2,29,128]{3,2,1,0:T(8,128)(2,1)S(1)}, u32[]{:S(2)}, u32[]{:S(2)}) collective-permute-start(bf16[4,2,29,128]{3,2,1,0:T(8,128)(2,1)S(1)} %dynamic-slice_bitcast_fusion.12), channel_id=1, source_target_pairs={{0,1},{1,0},{2,3},{3,2},{4,5},{5,4},{6,7},{7,6},{8,9},{9,8},{10,11... | collective-permute-start | bytes 178184 | tf_op jit(solution)/shard_map/ppermute | solution.py:557
  220.6 8.0 %collective-permute-start.46 = (bf16[4,56,896]{2,1,0:T(8,128)(2,1)S(1)}, bf16[4,56,896]{2,1,0:T(8,128)(2,1)}, u32[]{:S(2)}, u32[]{:S(2)}) collective-permute-start(bf16[4,56,896]{2,1,0:T(8,128)(2,1)S(1)} %dynamic-slice_bitcast_fusion.2), channel_id=1, source_target_pairs={{0,4},{2,6},{4,0},{6,2},{8,12},{10,14},{12,8},{14,10},{16,20},{18,... | collective-permute-start | bytes 1204232 | tf_op jit(solution)/shard_map/ppermute | solution.py:555
  223.1 49.2 %collective-permute-start.61 = (bf16[1,152,896]{2,1,0:T(8,128)(2,1)}, bf16[1,152,896]{2,1,0:T(8,128)(2,1)}, u32[]{:S(2)}, u32[]{:S(2)}) collective-permute-start(bf16[1,152,896]{2,1,0:T(8,128)(2,1)} %constant_dynamic-slice_fusion), channel_id=1, source_target_pairs={{0,16},{2,18},{4,20},{6,22},{8,24},{10,26},{12,28},{14,30},{16,0},... | collective-permute-start | bytes 817160 | tf_op jit(solution)/shard_map/ppermute | solution.py:719
  228.6 38.2 %collective-permute-start.52 = (bf16[1,224,1280]{2,1,0:T(8,128)(2,1)}, bf16[1,224,1280]{2,1,0:T(8,128)(2,1)}, u32[]{:S(2)}, u32[]{:S(2)}) collective-permute-start(bf16[1,224,1280]{2,1,0:T(8,128)(2,1)} %constant_dynamic-slice_fusion.1), channel_id=1, source_target_pairs={{0,16},{2,18},{4,20},{6,22},{8,24},{10,26},{12,28},{14,30},{16,0},... | collective-permute-start | bytes 1720328 | tf_op jit(solution)/shard_map/ppermute | solution.py:719
  233.3 53.2 %all-to-all-start = ((bf16[8,29,1024]{2,1,0:T(8,128)(2,1)}), bf16[8,29,1024]{2,1,0:T(8,128)(2,1)S(1)}, u32[]{:S(2)}, u32[]{:S(2)}) async-start(bf16[8,29,1024]{2,1,0:T(8,128)(2,1)} %pad_maximum_fusion.1.done_ref), calls=%async_computation | async-start | bytes 1048576 | tf_op jit(solution)/shard_map/all_to_all | solution.py:833
  272.3 7.8 %collective-permute-start.55 = (bf16[28,1280]{1,0:T(8,128)(2,1)S(1)}, bf16[28,1280]{1,0:T(8,128)(2,1)S(1)}, u32[]{:S(2)}, u32[]{:S(2)}) collective-permute-start(bf16[28,1280]{1,0:T(8,128)(2,1)S(1)} %get-tuple-element.122), channel_id=1, source_target_pairs={{0,3},{1,2},{2,1},{3,0},{4,7},{5,6},{6,5},{7,4},{8,11},{9,10},{10,... | collective-permute-start | bytes 215048 | tf_op jit(solution)/shard_map/ppermute | solution.py:558
  273.6 7.4 %collective-permute-start.56 = (bf16[28,1280]{1,0:T(8,128)(2,1)S(1)}, bf16[28,1280]{1,0:T(8,128)(2,1)S(1)}, u32[]{:S(2)}, u32[]{:S(2)}) collective-permute-start(bf16[28,1280]{1,0:T(8,128)(2,1)S(1)} %get-tuple-element.121), channel_id=1, source_target_pairs={{0,4},{2,6},{4,0},{6,2},{8,12},{10,14},{12,8},{14,10},{16,20},{18,... | collective-permute-start | bytes 215048 | tf_op jit(solution)/shard_map/ppermute | solution.py:555
  (62 other events, 334.3 us)
where the time goes:
time: 295 us; the launch traced here: 290 us
  waiting for transfers between devices  94.3 us (32%)
  starting transfers between devices  68.4 us (23%)
  Pallas kernels  53.7 us (18%)
  other arithmetic  34.8 us (12%)
  local copies, waits for them, and re-layouts  25.8 us (9%)
  matrix products  11.4 us (4%)
    ppermute x4, waiting for transfers between devices, z_half_send(): recv = lax.ppermute(send, CTX, [(i, i ^ mask) for i in range(ctx_count)])  47.3 us
    ppermute x38, starting transfers between devices, swap_of(): return lax.ppermute(a, CTX, [(i, i ^ cx) for i in range(ctx_count)])  32.9 us
    ppermute x38, waiting for transfers between devices, swap_of(): return lax.ppermute(a, CTX, [(i, i ^ cx) for i in range(ctx_count)])  24 us
    ppermute x11, waiting for transfers between devices, swap_of(): return lax.ppermute(a, 'wt', [(0, 1), (1, 0)])  23 us
    pallas_call x1, Pallas kernels, mlp(): pl.pallas_call(mlp_kernel, out_shape=(sds((4 * tok, dim), F32), sds((4 *...  14.1 us
    pallas_call x1, Pallas kernels, attention_bwd(): pl.pallas_call(functools.partial(bwd_kernel, pairs, groups, blk, 1.0 / ma...  11.7 us
    ppermute x11, starting transfers between devices, swap_of(): return lax.ppermute(a, 'wt', [(0, 1), (1, 0)])  11.7 us
    dot_general x10, matrix products, dot(): lax.dot_general(a, b, (((ca,), (cb,)), ((), ())), preferred_element_type=...  11.4 us
  transfers between devices with their start and end apart: 63, of which 16 were waited for; matrix products, arithmetic and copies ran while one was open for 20% of the time, Pallas kernels for 10%

commit v1 on v0

--- a/solution.py
+++ b/solution.py
@@ -354,22 +354,24 @@
             )
     for copy in copies:
         copy.start()
-    for m in range(2):
-        pieces = [None] * (ff_wide // 128)
-        for g in range(groups_z):
-            first = g * ff_blk // 128
-            lead = g * ff_blk - first * 128
-            tiles = -(-(lead + ff_blk) // 128)
+    pieces = [[None] * (ff_wide // 128) for _ in range(2)]
+    for g in range(groups_z):
+        first = g * ff_blk // 128
+        lead = g * ff_blk - first * 128
+        tiles = -(-(lead + ff_blk) // 128)
+        row = lax.broadcasted_iota(jnp.int32, (window, tiles * 128), 0)
+        lane = lax.broadcasted_iota(jnp.int32, (window, tiles * 128), 1) - lead
+        hot = jnp.logical_and(row == lane + shifts[g], jnp.logical_and(lane >= 0, lane < ff_blk))
+        hot = hot.astype(F32).astype(BF)
+        for m in range(2):
             copies[m * groups_z + g].wait()
-            row = lax.broadcasted_iota(jnp.int32, (window, tiles * 128), 0)
-            lane = lax.broadcasted_iota(jnp.int32, (window, tiles * 128), 1) - lead
-            hot = jnp.logical_and(row == lane + shifts[g], jnp.logical_and(lane >= 0, lane < ff_blk))
-            part = kdot(win[m * groups_z + g], hot.astype(F32).astype(BF), 1, 0)
+            part = kdot(win[m * groups_z + g], hot, 1, 0)
             for t in range(tiles):
                 tile = part[:, t * 128 : (t + 1) * 128]
-                old = pieces[first + t]
-                pieces[first + t] = tile if old is None else old + tile
-        for t, tile in enumerate(pieces):
+                old = pieces[m][first + t]
+                pieces[m][first + t] = tile if old is None else old + tile
+    for m in range(2):
+        for t, tile in enumerate(pieces[m]):
             col = m * ff_wide + t * 128
             out_ref[:, col : col + 128] = (
                 jnp.zeros((out_ref.shape[0], 128), BF) if tile is None else tile.astype(BF)
@@ -428,7 +430,7 @@
         down_w[2 * down_half :, :] = jnp.zeros((pad, down_w.shape[1]), BF)
 
     def chunk(start, out_ref, out_start):
-        rows = pl.ds(start, 2 * tok)
+        rows = pl.ds(start, 4 * tok)
         n2 = n2_all[rows, :]
         gate = kdot(n2, gu_w[:, :wide], 1, 0)
         up = kdot(n2, gu_w[:, wide:], 1, 0)
@@ -441,12 +443,10 @@
         g_ref[rows, :wide] = g_gate
         g_ref[rows, wide:] = g_up
         grad = kdot(g_gate, gu_w[:, :wide], 1, 1) + kdot(g_up, gu_w[:, wide:], 1, 1)
-        out_ref[pl.ds(out_start, 2 * tok), :] = grad.astype(out_ref.dtype)
-
-    for j in range(2):
-        chunk(2 * tok * (2 + j), send_ref, 2 * tok * j)
-    for j in range(2):
-        chunk(2 * tok * j, keep_ref, 2 * tok * j)
+        out_ref[pl.ds(out_start, 4 * tok), :] = grad.astype(out_ref.dtype)
+
+    chunk(4 * tok, send_ref, 0)
+    chunk(0, keep_ref, 0)
 
 
 def mlp(idx, n2, cot, gu, down):
@@ -502,6 +502,47 @@
     )(idx, att, gh, n1, gq)
 
 
+def kv_tail_kernel(count, core_rows, cos_ref, sin_ref, n1_ref, wq_ref, gn1_ref, *refs):
+    kv_refs = refs[:count]
+    keep_ref, send_ref, gw_ref, sum_ref = refs[count:]
+    total = kv_refs[0][...].astype(F32)
+    for ref in kv_refs[1:]:
+        total = total + ref[...].astype(F32)
+    lane = lax.broadcasted_iota(jnp.int32, total.shape, 1)
+    turned = jnp.where(lane < HD, total * sin_ref[:, : 2 * HD], 0.0)
+    ahead = pltpu.roll(turned, 2 * HD - HD // 2, 1)
+    behind = pltpu.roll(turned, HD // 2, 1)
+    turned = jnp.where(lane < HD // 2, ahead, jnp.where(lane < HD, -behind, 0.0))
+    grad = jnp.where(lane < HD, total * cos_ref[:, : 2 * HD], total) + turned
+    sum_ref[...] = jnp.sum(grad, axis=0, keepdims=True)
+    grad = grad.astype(BF)
+    cols = wq_ref.shape[1]
+    part = gn1_ref[...] + kdot(grad, wq_ref[:, cols - 2 * HD :], 1, 1)
+    for b in range(2):
+        at = slice(b * core_rows, (b + 1) * core_rows)
+        own = 2 * b * core_rows
+        keep_ref[at, :] = part[own : own + core_rows]
+        send_ref[at, :] = part[own + core_rows : own + 2 * core_rows]
+    gw_ref[...] = kdot(n1_ref[...], grad, 0, 0).astype(BF)
+
+
+def kv_tail(cosine, sine, n1, wq, gn1_q, kvs):
+    rows, dim = n1.shape
+    sds = jax.ShapeDtypeStruct
+    return pl.pallas_call(
+        functools.partial(kv_tail_kernel, len(kvs), rows // 4),
+        out_shape=(
+            sds((rows // 2, dim), F32),
+            sds((rows // 2, dim), F32),
+            sds((dim, 2 * HD), BF),
+            sds((1, 2 * HD), F32),
+        ),
+        in_specs=[VMEM_SPEC] * (5 + len(kvs)),
+        out_specs=(VMEM_SPEC,) * 4,
+        name="kv_tail",
+    )(cosine, sine, n1, wq, gn1_q, *kvs)
+
+
 def assemble_kernel(groups_z, ff_blk, ff_wide, factor, idx_ref, *refs):
     part_refs = refs[:8]
     gate_ref, up_ref, parts = refs[8:]
@@ -632,6 +673,7 @@
     cot_all = plane_gather(cot_own)
 
     z_odd = group & 1
+    gu_peer = ff_cols(plane ^ 1, z_odd, after(w_gate, wq_own), after(w_up, wq_own), half_dim // 2)
 
     def z_next_of(a):
         return lax.ppermute(a, CTX, [(i, i ^ 4) for i in range(ctx_count)])
@@ -663,20 +705,14 @@
         first, ahead, behind = halves(u)
         return u * cosine + jnp.where(first, -ahead, behind) * sine
 
-    def unrope(g):
-        cols = g.shape[1]
-        first, ahead, behind = halves(g * sine[:, :cols])
-        return g * cosine[:, :cols] + jnp.where(first, ahead, -behind)
-
     rotated = rope(project[:, :rope_cols]).astype(BF)
     q_scaled = rotated[:, :head_cols] * BF(1.0 / math.sqrt(HD))
     kv_own = jnp.concatenate([rotated[:, head_cols:], project[:, rope_cols:].astype(BF)], axis=1)
     kvs = [kv_own] + [swap_of(kv_own, 2 * k, 0) for k in range(1, pairs)]
 
-    w_gate_l, w_up_l = after(w_gate, kv_own), after(w_up, kv_own)
     w_down_l = after(w_down, kv_own)
     down_shape = (groups_z // 2, 8, ff_blk, dim)
-    gu_first = swap_of(ff_cols(plane ^ 1, z_odd, w_gate_l, w_up_l, half_dim // 2), 0, 1)
+    gu_first = swap_of(gu_peer, 0, 1)
     down_peer = w_down_l.reshape(2, -1, 8, ff_blk, dim)
     down_peer = pick(pick(down_peer, plane ^ 1, 2), z_odd).reshape(-1, dim)
     down_first = swap_of(down_peer, 0, 1)
@@ -763,16 +799,12 @@
     out_quad = plane_quad(out_keep, out_send)
     out_recv = plane_sends(out_quad)
 
-    dkv = dkv_recv[0].astype(F32)
-    for v in dkv_recv[1:]:
-        dkv = dkv + v.astype(F32)
-    gkv = jnp.concatenate([unrope(dkv[:, :HD]), dkv[:, HD:]], axis=1)
-    gkv_bf = gkv.astype(BF)
-    gn1_part = gn1_q + dot(gkv_bf, wq[:, head_cols:], 1, 1)
-    gn1_swap = swap_of(peer_rows(gn1_part), 1, 0)
-    gw_kv = dot(normed1_bf, gkv_bf, 0, 0, BF)
-    gb = jnp.concatenate([gq_sum[0], jnp.sum(gkv, axis=0)])
-    grad_norm1 = own_rows(gn1_part) + gn1_swap
+    gn1_keep, gn1_send, gw_kv, gkv_sum = kv_tail(
+        cosine, sine, normed1_bf, wq, gn1_q, dkv_recv
+    )
+    gn1_swap = swap_of(gn1_send, 1, 0)
+    gb = jnp.concatenate([gq_sum[0], gkv_sum[0]])
+    grad_norm1 = gn1_keep + gn1_swap
     x32 = x_own.astype(F32)
     inv1_own = own_rows(inv1)
     gg_attn = jnp.sum(grad_norm1 * x32 * inv1_own, axis=0)

time: 295 us -> 299 us (1.014)
  starting transfers between devices: 68.4 us -> 64.4 us
  Pallas kernels: 53.7 us -> 56.8 us
    ppermute x4, starting transfers between devices: 6.73 us -> 1.16 us  [z_half_send(): recv = lax.ppermute(send, CTX, [(i, i ^ mask) for i in range(ctx_count)])]
    ppermute x7, waiting for transfers between devices: 0.02 us -> 4.1 us  [swap_of(): lax.ppermute(a, CTX + ('wt',), [(i, i ^ 2 * cx + wx) for i in range(devic...]
    pallas_call x0 -> x1, Pallas kernels: none -> 3.59 us  [kv_tail(): pl.pallas_call(functools.partial(kv_tail_kernel, len(kvs), rows // 4), ou...]
    ppermute x38, waiting for transfers between devices: 24 us -> 20.7 us  [swap_of(): return lax.ppermute(a, CTX, [(i, i ^ cx) for i in range(ctx_count)])]
    dot_general x10 -> x8, matrix products: 11.4 us -> 12.7 us  [dot(): lax.dot_general(a, b, (((ca,), (cb,)), ((), ())), preferred_element_type=...]
    unnamed x94 -> x114, local copies, waits for them, and re-layouts: 5.08 us -> 6.07 us
  transfers between devices with their start and end apart: 63 -> 63, of which waited for: 16 -> 19; matrix products, arithmetic and copies ran while one was open for 20% -> 20% of each run, Pallas kernels for 10% -> 11%
where the time goes in v1:
time: 299 us; the launch traced here: 294 us
  waiting for transfers between devices  97.2 us (33%)
  starting transfers between devices  64.4 us (22%)
  Pallas kernels  56.8 us (19%)
  other arithmetic  32.5 us (11%)
  local copies, waits for them, and re-layouts  28.5 us (10%)
  matrix products  12.7 us (4%)
    ppermute x4, waiting for transfers between devices, z_half_send(): recv = lax.ppermute(send, CTX, [(i, i ^ mask) for i in range(ctx_count)])  46.5 us
    ppermute x38, starting transfers between devices, swap_of(): return lax.ppermute(a, CTX, [(i, i ^ cx) for i in range(ctx_count)])  31.8 us
    ppermute x11, waiting for transfers between devices, swap_of(): return lax.ppermute(a, 'wt', [(0, 1), (1, 0)])  23.7 us
    ppermute x38, waiting for transfers between devices, swap_of(): return lax.ppermute(a, CTX, [(i, i ^ cx) for i in range(ctx_count)])  20.7 us
    pallas_call x1, Pallas kernels, mlp(): pl.pallas_call(mlp_kernel, out_shape=(sds((4 * tok, dim), F32), sds((4 *...  13.5 us
    dot_general x8, matrix products, dot(): lax.dot_general(a, b, (((ca,), (cb,)), ((), ())), preferred_element_type=...  12.7 us
    ppermute x7, starting transfers between devices, swap_of(): lax.ppermute(a, CTX + ('wt',), [(i, i ^ 2 * cx + wx) for i in range(devic...  12.7 us
    ppermute x11, starting transfers between devices, swap_of(): return lax.ppermute(a, 'wt', [(0, 1), (1, 0)])  12.2 us
  transfers between devices with their start and end apart: 63, of which 19 were waited for; matrix products, arithmetic and copies ran while one was open for 20% of the time, Pallas kernels for 11%

profile of v1, /device:TPU:0, one launch (start us, length us, event | category | flops | bytes accessed | tf_op | source)
XLA Modules:
  0.0 294.0 jit_solution(5448109855228044351)
XLA Ops:
  4.5 2.6 collective-permute-start.1
  11.4 9.9 %collective-permute-done.1 = bf16[448,576]{1,0:T(8,128)(2,1)} collective-permute-done((bf16[448,576]{1,0:T(8,128)(2,1)}, bf16[448,576]{1,0:T(8,128)(2,1)}, u32[]{:S(2)}, u32[]{:S(2)}) %collective-permute-start.1) | collective-permute-done | bytes 516128 | tf_op jit(solution)/shard_map/ppermute | solution.py:598
  21.3 1.7 maximum_select_fusion.1.wq_ref
  24.5 2.1 collective-permute-start.2
  26.6 1.6 collective-permute-start.3
  28.8 3.0 %collective-permute-start.5 = (bf16[256,128]{1,0:T(8,128)(2,1)S(1)}, bf16[256,128]{1,0:T(8,128)(2,1)S(1)}, u32[]{:S(2)}, u32[]{:S(2)}) collective-permute-start(bf16[256,128]{1,0:T(8,128)(2,1)S(1)} %pad_maximum_fusion.7.refs_0_), channel_id=1, source_target_pairs={{0,16},{2,18},{4,20},{6,22},{8,24},{10,26},{12,28},{14,30},{16,0},... | collective-permute-start | bytes 196616 | tf_op jit(solution)/shard_map/ppermute | solution.py:596
  31.8 1.8 collective-permute-start.6
  33.6 3.0 %collective-permute-start.7 = (bf16[256,128]{1,0:T(8,128)(2,1)S(1)}, bf16[256,128]{1,0:T(8,128)(2,1)S(1)}, u32[]{:S(2)}, u32[]{:S(2)}) collective-permute-start(bf16[256,128]{1,0:T(8,128)(2,1)S(1)} %pad_maximum_fusion.7.refs_0_), channel_id=1, source_target_pairs={{0,24},{2,26},{4,28},{6,30},{8,16},{10,18},{12,20},{14,22},{16,8},... | collective-permute-start | bytes 196616 | tf_op jit(solution)/shard_map/ppermute | solution.py:596
  39.0 2.9 collective-permute-done.6.refs_5_
  42.1 2.4 collective-permute-start.21
  45.2 10.7 %attn_fwd.1 = (bf16[256,448]{1,0:T(8,128)(2,1)}, f32[2,1,896]{2,1,0:T(1,128)}) custom-call(s32[2]{0:T(128)} %pad_add_fusion.idx_ref, bf16[256,448]{1,0:T(8,128)(2,1)} %slice_multiply_fusion.1.q_ref, bf16[256,128]{1,0:T(8,128)(2,1)} %copy-done.18, bf16[256,128]{1,0:T(8,128)(2,1)} %copy-done.21, bf16[256,128]{1,0:T(8,128)(2,1)} %copy-done.22, ...), custom_call_target="tpu_custom_call" | custom-call | tf_op jit(solution)/shard_map/attn_fwd/pallas_call | solution.py:290
  56.5 4.8 %hidden_columns.3 = bf16[224,1280]{1,0:T(8,128)(2,1)} custom-call(s32[2]{0:T(128)} %pad_add_fusion.2.idx_ref, bf16[448,4864]{1,0:T(8,128)(2,1)} %gate_ref.1, bf16[448,4864]{1,0:T(8,128)(2,1)} %up_ref.1), custom_call_target="tpu_custom_call" | custom-call | tf_op jit(solution)/shard_map/hidden_columns/pallas_call | solution.py:384
  66.5 1.7 maximum_select_fusion.2
  71.3 7.3 %collective-permute-done.26.refs_17_ = bf16[224,1280]{1,0:T(8,128)(2,1)} collective-permute-done((bf16[224,1280]{1,0:T(8,128)(2,1)}, bf16[224,1280]{1,0:T(8,128)(2,1)}, u32[]{:S(2)}, u32[]{:S(2)}) %collective-permute-start.26) | collective-permute-done | bytes 573472 | tf_op jit(solution)/shard_map/ppermute | solution.py:598
  79.1 5.3 %collective-permute-done.28.refs_20_ = bf16[152,896]{1,0:T(8,128)(2,1)} collective-permute-done((bf16[152,896]{1,0:T(8,128)(2,1)S(1)}, bf16[152,896]{1,0:T(8,128)(2,1)}, u32[]{:S(2)}, u32[]{:S(2)}) %collective-permute-start.28) | collective-permute-done | bytes 272416 | tf_op jit(solution)/shard_map/ppermute | solution.py:598
  89.9 3.9 %collective-permute-done.14.refs_3_ = bf16[128,896]{1,0:T(8,128)(2,1)} collective-permute-done((bf16[128,896]{1,0:T(8,128)(2,1)}, bf16[128,896]{1,0:T(8,128)(2,1)}, u32[]{:S(2)}, u32[]{:S(2)}) %collective-permute-start.14) | collective-permute-done | bytes 229408 | tf_op jit(solution)/shard_map/ppermute | solution.py:599
  94.4 1.9 constant_dynamic-slice_fusion.2
  96.3 6.0 %hidden_columns.2.refs_16_ = bf16[448,1280]{1,0:T(8,128)(2,1)} custom-call(s32[2]{0:T(128)} %pad_add_fusion.1.idx_ref, bf16[448,4864]{1,0:T(8,128)(2,1)} %gate_ref.1, bf16[448,4864]{1,0:T(8,128)(2,1)} %up_ref.1), custom_call_target="tpu_custom_call" | custom-call | tf_op jit(solution)/shard_map/hidden_columns/pallas_call | solution.py:384
  103.4 2.1 collective-permute-done.29.refs_21_
  107.4 13.5 %mlp.1 = (f32[512,896]{1,0:T(8,128)}, bf16[512,896]{1,0:T(8,128)(2,1)}, bf16[1024,1280]{1,0:T(8,128)(2,1)}, bf16[1024,640]{1,0:T(8,128)(2,1)}, bf16[1024,896]{1,...) custom-call(s32[2]{0:T(128)} %pad_add_fusion.4.idx_ref, ...), custom_call_target="tpu_custom_call" | custom-call | tf_op jit(solution)/shard_map/mlp/pallas_call | solution.py:457
  121.2 2.5 fusion.9
  125.5 2.1 collective-permute-start.35
  129.1 1.6 fusion.73
  132.8 2.9 fusion.72
  140.4 1.8 fusion.57
  146.2 11.7 %attn_bwd.1 = (bf16[256,448]{1,0:T(8,128)(2,1)}, f32[1,448]{1,0:T(1,128)}, bf16[256,128]{1,0:T(8,128)(2,1)}, bf16[256,128]{1,0:T(8,128)(2,1)}, bf16[256,128]{1,0...) custom-call(s32[2]{0:T(128)} %pad_add_fusion.idx_ref, ...), custom_call_target="tpu_custom_call" | custom-call | tf_op jit(solution)/shard_map/attn_bwd/pallas_call | solution.py:315
  158.0 2.5 fusion.5.gn1_ref
  162.5 1.5 collective-permute-start.40
  164.0 2.4 collective-permute-start.41
  168.6 3.7 %outer_terms.1 = (bf16[8,56,896]{2,1,0:T(8,128)(2,1)}, bf16[8,56,896]{2,1,0:T(8,128)(2,1)}) custom-call(s32[2]{0:T(128)} %pad_add_fusion.3.idx_ref, bf16[256,896]{1,0:T(8,128)(2,1)} %copy-done.10, bf16[256,896]{1,0:T(8,128)(2,1)} %pad_maximum_fusion.4.gh_ref, bf16[256,896]{1,0:T(8,128)(2,1)} %copy-done.1, bf16[256,448]{1,0:T(8,128)(2,1)} %get-tuple-element.82.gq_ref), custom_call_target="tpu_custom_call" | custom-call | tf_op jit(solution)/shard_map/outer_terms/pallas_call | solution.py:496
  172.3 3.7 %collective-permute-start.43 = (bf16[256,128]{1,0:T(8,128)(2,1)S(1)}, bf16[256,128]{1,0:T(8,128)(2,1)S(1)}, u32[]{:S(2)}, u32[]{:S(2)}) collective-permute-start(bf16[256,128]{1,0:T(8,128)(2,1)S(1)} %copy-done.51), channel_id=1, source_target_pairs={{0,24},{2,26},{4,28},{6,30},{8,16},{10,18},{12,20},{14,22},{16,8},... | collective-permute-start | bytes 196616 | tf_op jit(solution)/shard_map/ppermute | solution.py:596
  176.4 2.1 collective-permute-start.50
  179.9 3.6 %collective-permute-done.44.refs_7_ = bf16[256,128]{1,0:T(8,128)(2,1)S(1)} collective-permute-done((bf16[256,128]{1,0:T(8,128)(2,1)S(1)}, bf16[256,128]{1,0:T(8,128)(2,1)S(1)}, u32[]{:S(2)}, u32[]{:S(2)}) %collective-permute-start.44) | collective-permute-done | bytes 65568 | tf_op jit(solution)/shard_map/ppermute | solution.py:596
  184.2 3.6 %kv_tail.1 = (f32[128,896]{1,0:T(8,128)}, f32[128,896]{1,0:T(8,128)}, bf16[896,128]{1,0:T(8,128)(2,1)}, f32[1,128]{1,0:T(1,128)}) custom-call(f32[256,512]{1,0:T(8,128)} %copy-done.3, f32[256,512]{1,0:T(8,128)} %copy-done.4, bf16[256,896]{1,0:T(8,128)(2,1)} %copy-done.1, bf16[896,576]{1,0:T(8,128)(2,1)} %copy-done, f32[256,896]{1,0:T(8,128)} %fusion.5.gn1_ref, ...), custom_call_target="tpu_custom_call" | custom-call | tf_op jit(solution)/shard_map/kv_tail/pallas_call | solution.py:532
  191.0 1.6 collective-permute-done.60
  198.1 2.9 collective-permute-done.47
  202.5 16.5 %collective-permute-done.51 = bf16[2,224,1280]{2,1,0:T(8,128)(2,1)} collective-permute-done((bf16[2,224,1280]{2,1,0:T(8,128)(2,1)}, bf16[2,224,1280]{2,1,0:T(8,128)(2,1)}, u32[]{:S(2)}, u32[]{:S(2)}) %collective-permute-start.51) | collective-permute-done | bytes 1146912 | tf_op jit(solution)/shard_map/ppermute | solution.py:755
  220.5 1.9 fusion
  223.2 1.6 add_convert_fusion
  228.4 5.6 %collective-permute-done.46.value_ref = bf16[4,56,896]{2,1,0:T(8,128)(2,1)} collective-permute-done((bf16[4,56,896]{2,1,0:T(8,128)(2,1)S(1)}, bf16[4,56,896]{2,1,0:T(8,128)(2,1)}, u32[]{:S(2)}, u32[]{:S(2)}) %collective-permute-start.46) | collective-permute-done | bytes 401440 | tf_op jit(solution)/shard_map/ppermute | solution.py:596
  236.3 4.5 %all-to-all-start = ((bf16[8,29,1024]{2,1,0:T(8,128)(2,1)}), bf16[8,29,1024]{2,1,0:T(8,128)(2,1)S(1)}, u32[]{:S(2)}, u32[]{:S(2)}) async-start(bf16[8,29,1024]{2,1,0:T(8,128)(2,1)} %pad_maximum_fusion.1.done_ref), calls=%async_computation | async-start | bytes 1048576 | tf_op jit(solution)/shard_map/all_to_all | solution.py:865
  241.8 28.4 %collective-permute-done.52.value_ref = bf16[1,224,1280]{2,1,0:T(8,128)(2,1)} collective-permute-done((bf16[1,224,1280]{2,1,0:T(8,128)(2,1)}, bf16[1,224,1280]{2,1,0:T(8,128)(2,1)}, u32[]{:S(2)}, u32[]{:S(2)}) %collective-permute-start.52) | collective-permute-done | bytes 573472 | tf_op jit(solution)/shard_map/ppermute | solution.py:755
  272.8 2.6 fusion.24
  275.4 1.6 collective-permute-start.55
  279.2 2.6 collective-permute-start.59
  281.7 1.8 multiply_bitcast_fusion
  283.8 2.9 collective-permute-done.58.refs_6_
  287.3 2.8 assemble.1
  (325 shorter events, 80.8 us)
Async XLA Ops:
  0.7 10.3 %collective-permute-start = (bf16[128,896]{1,0:T(8,128)(2,1)}, bf16[128,896]{1,0:T(8,128)(2,1)S(1)}, u32[]{:S(2)}, u32[]{:S(2)}) collective-permute-start(bf16[128,896]{1,0:T(8,128)(2,1)} %bitcast.141), channel_id=1, source_target_pairs={{0,2},{2,0},{4,6},{6,4},{8,10},{10,8},{12,14},{14,12},{16,18},{18,... | collective-permute-start | bytes 688136 | tf_op jit(solution)/shard_map/ppermute | solution.py:596
  4.5 16.7 %collective-permute-start.1 = (bf16[448,576]{1,0:T(8,128)(2,1)}, bf16[448,576]{1,0:T(8,128)(2,1)}, u32[]{:S(2)}, u32[]{:S(2)}) collective-permute-start(bf16[448,576]{1,0:T(8,128)(2,1)} %pad_maximum_fusion), channel_id=1, source_target_pairs={{0,1},{1,0},{2,3},{3,2},{4,5},{5,4},{6,7},{7,6},{8,9},{9,8},{10,11... | collective-permute-start | bytes 1548296 | tf_op jit(solution)/shard_map/ppermute | solution.py:598
  8.1 54.2 %collective-permute-start.10 = (bf16[448,448]{1,0:T(8,128)(2,1)}, bf16[448,448]{1,0:T(8,128)(2,1)}, u32[]{:S(2)}, u32[]{:S(2)}) collective-permute-start(bf16[448,448]{1,0:T(8,128)(2,1)} %constant_dynamic-slice_fusion.3), channel_id=1, source_target_pairs={{0,1},{1,0},{2,3},{3,2},{4,5},{5,4},{6,7},{7,6},{8,9},{9,8},{10,11... | collective-permute-start | bytes 1204232 | tf_op jit(solution)/shard_map/ppermute | solution.py:598
  28.2 8.5 %collective-permute-start.4 = (bf16[256,128]{1,0:T(8,128)(2,1)S(1)}, bf16[256,128]{1,0:T(8,128)(2,1)S(1)}, u32[]{:S(2)}, u32[]{:S(2)}) collective-permute-start(bf16[256,128]{1,0:T(8,128)(2,1)S(1)} %pad_maximum_fusion.7.refs_0_), channel_id=1, source_target_pairs={{0,12},{2,14},{4,8},{6,10},{8,4},{10,6},{12,0},{14,2},{16,28},{18,... | collective-permute-start | bytes 196616 | tf_op jit(solution)/shard_map/ppermute | solution.py:596
  28.8 8.8 %collective-permute-start.5 = (bf16[256,128]{1,0:T(8,128)(2,1)S(1)}, bf16[256,128]{1,0:T(8,128)(2,1)S(1)}, u32[]{:S(2)}, u32[]{:S(2)}) collective-permute-start(bf16[256,128]{1,0:T(8,128)(2,1)S(1)} %pad_maximum_fusion.7.refs_0_), channel_id=1, source_target_pairs={{0,16},{2,18},{4,20},{6,22},{8,24},{10,26},{12,28},{14,30},{16,0},... | collective-permute-start | bytes 196616 | tf_op jit(solution)/shard_map/ppermute | solution.py:596
  31.8 10.2 %collective-permute-start.6 = (bf16[256,128]{1,0:T(8,128)(2,1)S(1)}, bf16[256,128]{1,0:T(8,128)(2,1)S(1)}, u32[]{:S(2)}, u32[]{:S(2)}) collective-permute-start(bf16[256,128]{1,0:T(8,128)(2,1)S(1)} %pad_maximum_fusion.7.refs_0_), channel_id=1, source_target_pairs={{0,20},{2,22},{4,16},{6,18},{8,28},{10,30},{12,24},{14,26},{16,4},... | collective-permute-start | bytes 196616 | tf_op jit(solution)/shard_map/ppermute | solution.py:596
  33.6 8.5 %collective-permute-start.7 = (bf16[256,128]{1,0:T(8,128)(2,1)S(1)}, bf16[256,128]{1,0:T(8,128)(2,1)S(1)}, u32[]{:S(2)}, u32[]{:S(2)}) collective-permute-start(bf16[256,128]{1,0:T(8,128)(2,1)S(1)} %pad_maximum_fusion.7.refs_0_), channel_id=1, source_target_pairs={{0,24},{2,26},{4,28},{6,30},{8,16},{10,18},{12,20},{14,22},{16,8},... | collective-permute-start | bytes 196616 | tf_op jit(solution)/shard_map/ppermute | solution.py:596
  36.7 7.9 %collective-permute-start.8 = (bf16[256,128]{1,0:T(8,128)(2,1)S(1)}, bf16[256,128]{1,0:T(8,128)(2,1)S(1)}, u32[]{:S(2)}, u32[]{:S(2)}) collective-permute-start(bf16[256,128]{1,0:T(8,128)(2,1)S(1)} %pad_maximum_fusion.7.refs_0_), channel_id=1, source_target_pairs={{0,28},{2,30},{4,24},{6,26},{8,20},{10,22},{12,16},{14,18},{16,12}... | collective-permute-start | bytes 196616 | tf_op jit(solution)/shard_map/ppermute | solution.py:596
  37.5 31.9 %collective-permute-start.19 = (bf16[128,896]{1,0:T(8,128)(2,1)}, bf16[128,896]{1,0:T(8,128)(2,1)}, u32[]{:S(2)}, u32[]{:S(2)}) collective-permute-start(bf16[128,896]{1,0:T(8,128)(2,1)} %bitcast.12.refs_8_), channel_id=1, source_target_pairs={{0,1},{1,0},{2,3},{3,2},{4,5},{5,4},{6,7},{7,6},{8,9},{9,8},{10,11... | collective-permute-start | bytes 688136 | tf_op jit(solution)/shard_map/ppermute | solution.py:598
  41.9 28.4 %collective-permute-start.20 = (bf16[128,896]{1,0:T(8,128)(2,1)}, bf16[128,896]{1,0:T(8,128)(2,1)}, u32[]{:S(2)}, u32[]{:S(2)}) collective-permute-start(bf16[128,896]{1,0:T(8,128)(2,1)} %bitcast.12.refs_8_), channel_id=1, source_target_pairs={{0,4},{2,6},{4,0},{6,2},{8,12},{10,14},{12,8},{14,10},{16,20},{18,... | collective-permute-start | bytes 688136 | tf_op jit(solution)/shard_map/ppermute | solution.py:596
  42.1 43.4 %collective-permute-start.21 = (bf16[128,896]{1,0:T(8,128)(2,1)}, bf16[128,896]{1,0:T(8,128)(2,1)}, u32[]{:S(2)}, u32[]{:S(2)}) collective-permute-start(bf16[128,896]{1,0:T(8,128)(2,1)} %bitcast.12.refs_8_), channel_id=1, source_target_pairs={{0,5},{1,4},{2,7},{3,6},{4,1},{5,0},{6,3},{7,2},{8,13},{9,12},{10,... | collective-permute-start | bytes 688136 | tf_op jit(solution)/shard_map/ppermute | solution.py:599
  55.9 7.5 %collective-permute-start.9 = (bf16[256,448]{1,0:T(8,128)(2,1)}, bf16[256,448]{1,0:T(8,128)(2,1)S(1)}, u32[]{:S(2)}, u32[]{:S(2)}) collective-permute-start(bf16[256,448]{1,0:T(8,128)(2,1)} %get-tuple-element.57.att_ref), channel_id=1, source_target_pairs={{0,2},{2,0},{4,6},{6,4},{8,10},{10,8},{12,14},{14,12},{16,18},{18,... | collective-permute-start | bytes 688136 | tf_op jit(solution)/shard_map/ppermute | solution.py:596
  62.4 16.2 %collective-permute-start.26 = (bf16[224,1280]{1,0:T(8,128)(2,1)}, bf16[224,1280]{1,0:T(8,128)(2,1)}, u32[]{:S(2)}, u32[]{:S(2)}) collective-permute-start(bf16[224,1280]{1,0:T(8,128)(2,1)} %hidden_columns.3), channel_id=1, source_target_pairs={{0,1},{1,0},{2,3},{3,2},{4,5},{5,4},{6,7},{7,6},{8,9},{9,8},{10,11... | collective-permute-start | bytes 1720328 | tf_op jit(solution)/shard_map/ppermute | solution.py:598
  65.4 19.0 %collective-permute-start.28 = (bf16[152,896]{1,0:T(8,128)(2,1)S(1)}, bf16[152,896]{1,0:T(8,128)(2,1)}, u32[]{:S(2)}, u32[]{:S(2)}) collective-permute-start(bf16[152,896]{1,0:T(8,128)(2,1)S(1)} %dynamic-slice_bitcast_fusion.3), channel_id=1, source_target_pairs={{0,1},{1,0},{2,3},{3,2},{4,5},{5,4},{6,7},{7,6},{8,9},{9,8},{10,11... | collective-permute-start | bytes 817160 | tf_op jit(solution)/shard_map/ppermute | solution.py:598
  69.4 17.1 %collective-permute-start.22 = (bf16[128,896]{1,0:T(8,128)(2,1)}, bf16[128,896]{1,0:T(8,128)(2,1)}, u32[]{:S(2)}, u32[]{:S(2)}) collective-permute-start(bf16[128,896]{1,0:T(8,128)(2,1)} %bitcast.12.refs_8_), channel_id=1, source_target_pairs={{0,2},{2,0},{4,6},{6,4},{8,10},{10,8},{12,14},{14,12},{16,18},{18,... | collective-permute-start | bytes 688136 | tf_op jit(solution)/shard_map/ppermute | solution.py:596
  70.3 19.0 %collective-permute-start.12 = (bf16[128,896]{1,0:T(8,128)(2,1)}, bf16[128,896]{1,0:T(8,128)(2,1)}, u32[]{:S(2)}, u32[]{:S(2)}) collective-permute-start(bf16[128,896]{1,0:T(8,128)(2,1)} %multiply_convert_fusion.refs_0_), channel_id=1, source_target_pairs={{0,1},{1,0},{2,3},{3,2},{4,5},{5,4},{6,7},{7,6},{8,9},{9,8},{10,11... | collective-permute-start | bytes 688136 | tf_op jit(solution)/shard_map/ppermute | solution.py:598
  78.6 10.8 %collective-permute-start.13 = (bf16[128,896]{1,0:T(8,128)(2,1)}, bf16[128,896]{1,0:T(8,128)(2,1)}, u32[]{:S(2)}, u32[]{:S(2)}) collective-permute-start(bf16[128,896]{1,0:T(8,128)(2,1)} %multiply_convert_fusion.refs_0_), channel_id=1, source_target_pairs={{0,4},{2,6},{4,0},{6,2},{8,12},{10,14},{12,8},{14,10},{16,20},{18,... | collective-permute-start | bytes 688136 | tf_op jit(solution)/shard_map/ppermute | solution.py:596
  84.4 9.4 %collective-permute-start.14 = (bf16[128,896]{1,0:T(8,128)(2,1)}, bf16[128,896]{1,0:T(8,128)(2,1)}, u32[]{:S(2)}, u32[]{:S(2)}) collective-permute-start(bf16[128,896]{1,0:T(8,128)(2,1)} %multiply_convert_fusion.refs_0_), channel_id=1, source_target_pairs={{0,5},{1,4},{2,7},{3,6},{4,1},{5,0},{6,3},{7,2},{8,13},{9,12},{10,... | collective-permute-start | bytes 688136 | tf_op jit(solution)/shard_map/ppermute | solution.py:599
  85.5 21.2 %collective-permute-start.27 = (bf16[224,1280]{1,0:T(8,128)(2,1)}, bf16[224,1280]{1,0:T(8,128)(2,1)}, u32[]{:S(2)}, u32[]{:S(2)}) collective-permute-start(bf16[224,1280]{1,0:T(8,128)(2,1)} %collective-permute-done.26.refs_17_), channel_id=1, source_target_pairs={{0,8},{2,10},{4,12},{6,14},{8,0},{10,2},{12,4},{14,6},{16,24},{18,... | collective-permute-start | bytes 1720328 | tf_op jit(solution)/shard_map/ppermute | solution.py:679
  86.5 19.0 %collective-permute-start.29 = (bf16[152,896]{1,0:T(8,128)(2,1)}, bf16[152,896]{1,0:T(8,128)(2,1)}, u32[]{:S(2)}, u32[]{:S(2)}) collective-permute-start(bf16[152,896]{1,0:T(8,128)(2,1)} %collective-permute-done.28.refs_20_), channel_id=1, source_target_pairs={{0,8},{2,10},{4,12},{6,14},{8,0},{10,2},{12,4},{14,6},{16,24},{18,... | collective-permute-start | bytes 817160 | tf_op jit(solution)/shard_map/ppermute | solution.py:679
  89.3 13.0 %collective-permute-start.23 = (bf16[128,896]{1,0:T(8,128)(2,1)}, bf16[128,896]{1,0:T(8,128)(2,1)}, u32[]{:S(2)}, u32[]{:S(2)}) collective-permute-start(bf16[128,896]{1,0:T(8,128)(2,1)} %collective-permute-done.19.refs_9_), channel_id=1, source_target_pairs={{0,2},{2,0},{4,6},{6,4},{8,10},{10,8},{12,14},{14,12},{16,18},{18,... | collective-permute-start | bytes 688136 | tf_op jit(solution)/shard_map/ppermute | solution.py:596
  89.3 13.6 %collective-permute-start.24 = (bf16[128,896]{1,0:T(8,128)(2,1)}, bf16[128,896]{1,0:T(8,128)(2,1)}, u32[]{:S(2)}, u32[]{:S(2)}) collective-permute-start(bf16[128,896]{1,0:T(8,128)(2,1)} %collective-permute-done.20.refs_10_), channel_id=1, source_target_pairs={{0,2},{2,0},{4,6},{6,4},{8,10},{10,8},{12,14},{14,12},{16,18},{18,... | collective-permute-start | bytes 688136 | tf_op jit(solution)/shard_map/ppermute | solution.py:596
  93.8 9.2 %collective-permute-start.25 = (bf16[128,896]{1,0:T(8,128)(2,1)}, bf16[128,896]{1,0:T(8,128)(2,1)}, u32[]{:S(2)}, u32[]{:S(2)}) collective-permute-start(bf16[128,896]{1,0:T(8,128)(2,1)} %collective-permute-done.21.refs_11_), channel_id=1, source_target_pairs={{0,2},{2,0},{4,6},{6,4},{8,10},{10,8},{12,14},{14,12},{16,18},{18,... | collective-permute-start | bytes 688136 | tf_op jit(solution)/shard_map/ppermute | solution.py:596
  123.8 13.1 %collective-permute-start.30 = (bf16[512,896]{1,0:T(8,128)(2,1)S(1)}, bf16[512,896]{1,0:T(8,128)(2,1)S(1)}, u32[]{:S(2)}, u32[]{:S(2)}) collective-permute-start(bf16[512,896]{1,0:T(8,128)(2,1)S(1)} %fusion.9), channel_id=1, source_target_pairs={{0,2},{2,0},{4,6},{6,4},{8,10},{10,8},{12,14},{14,12},{16,18},{18,... | collective-permute-start | bytes 2752520 | tf_op jit(solution)/shard_map/ppermute | solution.py:596
  125.5 13.9 %collective-permute-start.35 = (bf16[128,896]{1,0:T(8,128)(2,1)S(1)}, bf16[128,896]{1,0:T(8,128)(2,1)S(1)}, u32[]{:S(2)}, u32[]{:S(2)}) collective-permute-start(bf16[128,896]{1,0:T(8,128)(2,1)S(1)} %get-tuple-element.117), channel_id=1, source_target_pairs={{0,5},{1,4},{2,7},{3,6},{4,1},{5,0},{6,3},{7,2},{8,13},{9,12},{10,... | collective-permute-start | bytes 688136 | tf_op jit(solution)/shard_map/ppermute | solution.py:599
  127.6 11.8 %collective-permute-start.34 = (bf16[128,896]{1,0:T(8,128)(2,1)S(1)}, bf16[128,896]{1,0:T(8,128)(2,1)S(1)}, u32[]{:S(2)}, u32[]{:S(2)}) collective-permute-start(bf16[128,896]{1,0:T(8,128)(2,1)S(1)} %get-tuple-element.118), channel_id=1, source_target_pairs={{0,4},{2,6},{4,0},{6,2},{8,12},{10,14},{12,8},{14,10},{16,20},{18,... | collective-permute-start | bytes 688136 | tf_op jit(solution)/shard_map/ppermute | solution.py:596
  128.1 11.2 %collective-permute-start.33 = (bf16[128,896]{1,0:T(8,128)(2,1)S(1)}, bf16[128,896]{1,0:T(8,128)(2,1)S(1)}, u32[]{:S(2)}, u32[]{:S(2)}) collective-permute-start(bf16[128,896]{1,0:T(8,128)(2,1)S(1)} %get-tuple-element.116), channel_id=1, source_target_pairs={{0,1},{1,0},{2,3},{3,2},{4,5},{5,4},{6,7},{7,6},{8,9},{9,8},{10,11... | collective-permute-start | bytes 688136 | tf_op jit(solution)/shard_map/ppermute | solution.py:598
  160.5 11.8 %collective-permute-start.38 = (bf16[256,128]{1,0:T(8,128)(2,1)S(1)}, bf16[256,128]{1,0:T(8,128)(2,1)S(1)}, u32[]{:S(2)}, u32[]{:S(2)}) collective-permute-start(bf16[256,128]{1,0:T(8,128)(2,1)S(1)} %copy-done.56), channel_id=1, source_target_pairs={{0,4},{2,6},{4,0},{6,2},{8,12},{10,14},{12,8},{14,10},{16,20},{18,... | collective-permute-start | bytes 196616 | tf_op jit(solution)/shard_map/ppermute | solution.py:596
  161.9 14.1 %collective-permute-start.39 = (bf16[256,128]{1,0:T(8,128)(2,1)S(1)}, bf16[256,128]{1,0:T(8,128)(2,1)S(1)}, u32[]{:S(2)}, u32[]{:S(2)}) collective-permute-start(bf16[256,128]{1,0:T(8,128)(2,1)S(1)} %copy-done.55), channel_id=1, source_target_pairs={{0,8},{2,10},{4,12},{6,14},{8,0},{10,2},{12,4},{14,6},{16,24},{18,... | collective-permute-start | bytes 196616 | tf_op jit(solution)/shard_map/ppermute | solution.py:596
  162.5 13.9 %collective-permute-start.40 = (bf16[256,128]{1,0:T(8,128)(2,1)S(1)}, bf16[256,128]{1,0:T(8,128)(2,1)S(1)}, u32[]{:S(2)}, u32[]{:S(2)}) collective-permute-start(bf16[256,128]{1,0:T(8,128)(2,1)S(1)} %copy-done.54), channel_id=1, source_target_pairs={{0,12},{2,14},{4,8},{6,10},{8,4},{10,6},{12,0},{14,2},{16,28},{18,... | collective-permute-start | bytes 196616 | tf_op jit(solution)/shard_map/ppermute | solution.py:596
  164.0 14.5 %collective-permute-start.41 = (bf16[256,128]{1,0:T(8,128)(2,1)S(1)}, bf16[256,128]{1,0:T(8,128)(2,1)S(1)}, u32[]{:S(2)}, u32[]{:S(2)}) collective-permute-start(bf16[256,128]{1,0:T(8,128)(2,1)S(1)} %copy-done.53), channel_id=1, source_target_pairs={{0,16},{2,18},{4,20},{6,22},{8,24},{10,26},{12,28},{14,30},{16,0},... | collective-permute-start | bytes 196616 | tf_op jit(solution)/shard_map/ppermute | solution.py:596
  166.5 12.8 %collective-permute-start.42 = (bf16[256,128]{1,0:T(8,128)(2,1)S(1)}, bf16[256,128]{1,0:T(8,128)(2,1)S(1)}, u32[]{:S(2)}, u32[]{:S(2)}) collective-permute-start(bf16[256,128]{1,0:T(8,128)(2,1)S(1)} %copy-done.52), channel_id=1, source_target_pairs={{0,20},{2,22},{4,16},{6,18},{8,28},{10,30},{12,24},{14,26},{16,4},... | collective-permute-start | bytes 196616 | tf_op jit(solution)/shard_map/ppermute | solution.py:596
  172.3 7.7 %collective-permute-start.43 = (bf16[256,128]{1,0:T(8,128)(2,1)S(1)}, bf16[256,128]{1,0:T(8,128)(2,1)S(1)}, u32[]{:S(2)}, u32[]{:S(2)}) collective-permute-start(bf16[256,128]{1,0:T(8,128)(2,1)S(1)} %copy-done.51), channel_id=1, source_target_pairs={{0,24},{2,26},{4,28},{6,30},{8,16},{10,18},{12,20},{14,22},{16,8},... | collective-permute-start | bytes 196616 | tf_op jit(solution)/shard_map/ppermute | solution.py:596
  176.0 7.5 %collective-permute-start.44 = (bf16[256,128]{1,0:T(8,128)(2,1)S(1)}, bf16[256,128]{1,0:T(8,128)(2,1)S(1)}, u32[]{:S(2)}, u32[]{:S(2)}) collective-permute-start(bf16[256,128]{1,0:T(8,128)(2,1)S(1)} %copy-done.50), channel_id=1, source_target_pairs={{0,28},{2,30},{4,24},{6,26},{8,20},{10,22},{12,16},{14,18},{16,12}... | collective-permute-start | bytes 196616 | tf_op jit(solution)/shard_map/ppermute | solution.py:596
  176.4 96.4 %collective-permute-start.50 = (bf16[128,896]{1,0:T(8,128)(2,1)}, bf16[128,896]{1,0:T(8,128)(2,1)}, u32[]{:S(2)}, u32[]{:S(2)}) collective-permute-start(bf16[128,896]{1,0:T(8,128)(2,1)} %get-tuple-element.120), channel_id=1, source_target_pairs={{0,5},{1,4},{2,7},{3,6},{4,1},{5,0},{6,3},{7,2},{8,13},{9,12},{10,... | collective-permute-start | bytes 688136 | tf_op jit(solution)/shard_map/ppermute | solution.py:599
  178.6 94.2 %collective-permute-start.49 = (bf16[128,896]{1,0:T(8,128)(2,1)}, bf16[128,896]{1,0:T(8,128)(2,1)}, u32[]{:S(2)}, u32[]{:S(2)}) collective-permute-start(bf16[128,896]{1,0:T(8,128)(2,1)} %get-tuple-element.121), channel_id=1, source_target_pairs={{0,4},{2,6},{4,0},{6,2},{8,12},{10,14},{12,8},{14,10},{16,20},{18,... | collective-permute-start | bytes 688136 | tf_op jit(solution)/shard_map/ppermute | solution.py:596
  179.2 61.6 %collective-permute-start.31 = (bf16[128,896]{1,0:T(8,128)(2,1)}, bf16[128,896]{1,0:T(8,128)(2,1)}, u32[]{:S(2)}, u32[]{:S(2)}) collective-permute-start(bf16[128,896]{1,0:T(8,128)(2,1)} %get-tuple-element.119), channel_id=1, source_target_pairs={{0,1},{1,0},{2,3},{3,2},{4,5},{5,4},{6,7},{7,6},{8,9},{9,8},{10,11... | collective-permute-start | bytes 688136 | tf_op jit(solution)/shard_map/ppermute | solution.py:598
  179.9 12.6 %collective-permute-start.60 = (bf16[2,152,896]{2,1,0:T(8,128)(2,1)}, bf16[2,152,896]{2,1,0:T(8,128)(2,1)S(1)}, u32[]{:S(2)}, u32[]{:S(2)}) collective-permute-start(bf16[2,152,896]{2,1,0:T(8,128)(2,1)} %dynamic-slice_bitcast_fusion.1), channel_id=1, source_target_pairs={{0,8},{2,10},{4,12},{6,14},{8,0},{10,2},{12,4},{14,6},{16,24},{18,... | collective-permute-start | bytes 1634312 | tf_op jit(solution)/shard_map/ppermute | solution.py:755
  192.6 26.5 %collective-permute-start.51 = (bf16[2,224,1280]{2,1,0:T(8,128)(2,1)}, bf16[2,224,1280]{2,1,0:T(8,128)(2,1)}, u32[]{:S(2)}, u32[]{:S(2)}) collective-permute-start(bf16[2,224,1280]{2,1,0:T(8,128)(2,1)} %dynamic-slice_bitcast_fusion), channel_id=1, source_target_pairs={{0,8},{2,10},{4,12},{6,14},{8,0},{10,2},{12,4},{14,6},{16,24},{18,... | collective-permute-start | bytes 3440648 | tf_op jit(solution)/shard_map/ppermute | solution.py:755
  201.0 21.4 %collective-permute-start.37 = (bf16[8,56,896]{2,1,0:T(8,128)(2,1)}, bf16[8,56,896]{2,1,0:T(8,128)(2,1)S(1)}, u32[]{:S(2)}, u32[]{:S(2)}) collective-permute-start(bf16[8,56,896]{2,1,0:T(8,128)(2,1)} %get-tuple-element.84), channel_id=1, source_target_pairs={{0,1},{1,0},{2,3},{3,2},{4,5},{5,4},{6,7},{7,6},{8,9},{9,8},{10,11... | collective-permute-start | bytes 2408456 | tf_op jit(solution)/shard_map/ppermute | solution.py:598
  219.0 7.7 %collective-permute-start.48 = (bf16[4,2,29,128]{3,2,1,0:T(8,128)(2,1)S(1)}, bf16[4,2,29,128]{3,2,1,0:T(8,128)(2,1)S(1)}, u32[]{:S(2)}, u32[]{:S(2)}) collective-permute-start(bf16[4,2,29,128]{3,2,1,0:T(8,128)(2,1)S(1)} %dynamic-slice_bitcast_fusion.12), channel_id=1, source_target_pairs={{0,1},{1,0},{2,3},{3,2},{4,5},{5,4},{6,7},{7,6},{8,9},{9,8},{10,11... | collective-permute-start | bytes 178184 | tf_op jit(solution)/shard_map/ppermute | solution.py:598
  224.9 9.2 %collective-permute-start.46 = (bf16[4,56,896]{2,1,0:T(8,128)(2,1)S(1)}, bf16[4,56,896]{2,1,0:T(8,128)(2,1)}, u32[]{:S(2)}, u32[]{:S(2)}) collective-permute-start(bf16[4,56,896]{2,1,0:T(8,128)(2,1)S(1)} %dynamic-slice_bitcast_fusion.2), channel_id=1, source_target_pairs={{0,4},{2,6},{4,0},{6,2},{8,12},{10,14},{12,8},{14,10},{16,20},{18,... | collective-permute-start | bytes 1204232 | tf_op jit(solution)/shard_map/ppermute | solution.py:596
  226.7 48.7 %collective-permute-start.61 = (bf16[1,152,896]{2,1,0:T(8,128)(2,1)}, bf16[1,152,896]{2,1,0:T(8,128)(2,1)}, u32[]{:S(2)}, u32[]{:S(2)}) collective-permute-start(bf16[1,152,896]{2,1,0:T(8,128)(2,1)} %constant_dynamic-slice_fusion), channel_id=1, source_target_pairs={{0,16},{2,18},{4,20},{6,22},{8,24},{10,26},{12,28},{14,30},{16,0},... | collective-permute-start | bytes 817160 | tf_op jit(solution)/shard_map/ppermute | solution.py:755
  234.0 36.2 %collective-permute-start.52 = (bf16[1,224,1280]{2,1,0:T(8,128)(2,1)}, bf16[1,224,1280]{2,1,0:T(8,128)(2,1)}, u32[]{:S(2)}, u32[]{:S(2)}) collective-permute-start(bf16[1,224,1280]{2,1,0:T(8,128)(2,1)} %constant_dynamic-slice_fusion.1), channel_id=1, source_target_pairs={{0,16},{2,18},{4,20},{6,22},{8,24},{10,26},{12,28},{14,30},{16,0},... | collective-permute-start | bytes 1720328 | tf_op jit(solution)/shard_map/ppermute | solution.py:755
  236.3 53.8 %all-to-all-start = ((bf16[8,29,1024]{2,1,0:T(8,128)(2,1)}), bf16[8,29,1024]{2,1,0:T(8,128)(2,1)S(1)}, u32[]{:S(2)}, u32[]{:S(2)}) async-start(bf16[8,29,1024]{2,1,0:T(8,128)(2,1)} %pad_maximum_fusion.1.done_ref), calls=%async_computation | async-start | bytes 1048576 | tf_op jit(solution)/shard_map/all_to_all | solution.py:865
  275.4 8.1 %collective-permute-start.55 = (bf16[28,1280]{1,0:T(8,128)(2,1)S(1)}, bf16[28,1280]{1,0:T(8,128)(2,1)S(1)}, u32[]{:S(2)}, u32[]{:S(2)}) collective-permute-start(bf16[28,1280]{1,0:T(8,128)(2,1)S(1)} %get-tuple-element.126), channel_id=1, source_target_pairs={{0,3},{1,2},{2,1},{3,0},{4,7},{5,6},{6,5},{7,4},{8,11},{9,10},{10,... | collective-permute-start | bytes 215048 | tf_op jit(solution)/shard_map/ppermute | solution.py:599
  279.0 7.6 %collective-permute-start.58 = (bf16[28,1280]{1,0:T(8,128)(2,1)S(1)}, bf16[28,1280]{1,0:T(8,128)(2,1)S(1)}, u32[]{:S(2)}, u32[]{:S(2)}) collective-permute-start(bf16[28,1280]{1,0:T(8,128)(2,1)S(1)} %get-tuple-element.123), channel_id=1, source_target_pairs={{0,6},{2,4},{4,2},{6,0},{8,14},{10,12},{12,10},{14,8},{16,22},{18,... | collective-permute-start | bytes 215048 | tf_op jit(solution)/shard_map/ppermute | solution.py:596
  279.2 7.5 %collective-permute-start.59 = (bf16[28,1280]{1,0:T(8,128)(2,1)S(1)}, bf16[28,1280]{1,0:T(8,128)(2,1)S(1)}, u32[]{:S(2)}, u32[]{:S(2)}) collective-permute-start(bf16[28,1280]{1,0:T(8,128)(2,1)S(1)} %get-tuple-element.122), channel_id=1, source_target_pairs={{0,7},{1,6},{2,5},{3,4},{4,3},{5,2},{6,1},{7,0},{8,15},{9,14},{10,... | collective-permute-start | bytes 215048 | tf_op jit(solution)/shard_map/ppermute | solution.py:599
  (72 other events, 515.5 us)
